TPU v7x, 32 devices: a whole 2x2x4 slice. The times are simulated.
32 devices in a mesh: seq: 4 (over x, core), head: 8 (over z, y).
Axes of the slice: x: 2, y: 2, z: 4, core: 2. Of those that a mesh axis runs over, the one named last changes fastest.
Arguments:
- tokens: bfloat16 [1024, 4096], P('seq', 'head'), may hold values from -6 to 6
- w_query: bfloat16 [4096, 2048], P(None, 'head'), may hold values from -0.09375 to 0.09375
- w_key: bfloat16 [4096, 2048], P(None, 'head'), may hold values from -0.09375 to 0.09375
- w_value: bfloat16 [4096, 2048], P(None, 'head'), may hold values from -0.09375 to 0.09375
- w_out: bfloat16 [2048, 4096], P('head'), may hold values from -0.125 to 0.125
- grad_out: bfloat16 [1024, 4096], P('seq', 'head'), may hold values from -6 to 6
- state_in: float32 [16, 128, 128], P('head'), may hold values from -384 to 384
Outputs:
- result: bfloat16 [1024, 4096], P('seq', 'head')
- grad_tokens: float32 [1024, 4096], P('seq', 'head')
- grad_wq: float32 [4096, 2048], P('seq', 'head')
- grad_wk: float32 [4096, 2048], P('seq', 'head')
- grad_wv: float32 [4096, 2048], P('seq', 'head')
- grad_wo: float32 [2048, 4096], P('head', 'seq')
- grad_state_in: float32 [16, 128, 128], P('head')
All inputs are finite; a program needn't handle non-finite values.
Results may differ from a plain program's by a relative error of at most 0.018.
Values may be sent and summed in bfloat16 or wider, within the bound.
A program may use at most 64 MiB of HBM per device.

v0:
```python
import jax
import jax.numpy as jnp
from jax import lax
from jax.experimental import pallas as pl
from jax.experimental.pallas import tpu as pltpu
from jax.sharding import PartitionSpec as P

DH = 128
BLOCK = 256
EPSILON = 1e-06
WIDE = jnp.float32
HALF = jnp.bfloat16
MESH = pl.DeviceIdType.MESH
NN = (((1,), (0,)), ((), ()))
NT = (((1,), (1,)), ((), ()))
TN = (((0,), (0,)), ((), ()))


def mul(left, right, dims=NN):
    return lax.dot_general(left, right, dims, preferred_element_type=WIDE)


def inner_size(count):
    inner = 1
    while 4 * inner * inner <= count:
        inner *= 2
    return inner


class Line:
    def __init__(self, place, size, device):
        self.place, self.size, self.device = place, size, device

    def has(self, way):
        return self.place < self.size - 1 if way == 0 else self.place > 0

    def next(self, way):
        return self.device(self.place + (1 if way == 0 else -1))


class Gather:
    def __init__(self, source, slots, recv, sent_outer, sent_inner, outer, inner, cut, seen):
        self.source, self.slots, self.recv = source, slots, recv
        self.sent_outer, self.sent_inner = sent_outer, sent_inner
        self.outer, self.inner, self.seen = outer, inner, seen
        rows = slots.shape[1]
        self.parts = [part for part in ((0, 0, cut), (1, cut, rows - cut)) if part[2]]

    def slot(self, place_outer, place_inner):
        return place_outer * self.inner.size + place_inner

    def copy(self, part, slot, line, way, source=None):
        number, start, rows = part
        sent = self.sent_outer if line is self.outer else self.sent_inner
        piece = self.slots.at[slot, pl.ds(start, rows)]
        return pltpu.make_async_remote_copy(
            src_ref=piece if source is None else source.at[pl.ds(start, rows)],
            dst_ref=piece,
            send_sem=sent.at[number, slot, way],
            recv_sem=self.recv.at[number, slot],
            device_id=line.next(way),
            device_id_type=MESH,
        )

    def send(self, part, slot, line, way, also=True, source=None):
        @pl.when(line.has(way) & also)
        def _():
            self.copy(part, slot, line, way, source).start()

    def arrive(self, part, slot):
        number, start, rows = part
        piece = self.slots.at[slot, pl.ds(start, rows)]
        pltpu.make_async_copy(piece, piece, self.recv.at[number, slot]).wait()

    def own(self, line):
        slot = self.slot(self.outer.place, self.inner.place)
        for part in self.parts:
            for way in (0, 1):
                self.send(part, slot, line, way, source=self.source)

    def cross_row(self):
        for part in self.parts[1:]:
            for way in (0, 1):
                for step in range(1, self.inner.size):
                    place = self.inner.place + (-step if way == 0 else step)

                    @pl.when((place >= 0) & (place < self.inner.size))
                    def _():
                        slot = self.slot(self.outer.place, place)
                        self.arrive(part, slot)
                        self.send(part, slot, self.inner, way)
                        self.send(part, slot, self.outer, 0)
                        self.send(part, slot, self.outer, 1)

    def from_outer(self, distance):
        @pl.loop(0, 2)
        def _(side):
            place = self.outer.place + (2 * side - 1) * distance

            @pl.when((place >= 0) & (place < self.outer.size))
            def _():
                mine = self.slot(place, self.inner.place)
                for part in self.parts:
                    owners = [self.inner.place] if part[0] == 0 else range(self.inner.size)
                    for owner in owners:
                        slot = self.slot(place, owner)
                        self.arrive(part, slot)
                        self.send(part, slot, self.outer, 0, side == 0)
                        self.send(part, slot, self.outer, 1, side == 1)
                    if part[0] == 0:
                        self.send(part, mine, self.inner, 0)
                        self.send(part, mine, self.inner, 1)
                self.seen(mine)

    def from_inner(self, distance):
        @pl.loop(0, 2)
        def _(side):
            row = self.outer.place + (2 * side - 1) * distance

            @pl.when((row >= 0) & (row < self.outer.size) & ((distance > 0) | (side == 0)))
            def _():
                @pl.loop(0, 2)
                def _(way):
                    @pl.loop(1, self.inner.size)
                    def _(step):
                        place = self.inner.place + (2 * way - 1) * step

                        @pl.when((place >= 0) & (place < self.inner.size))
                        def _():
                            slot = self.slot(row, place)
                            self.arrive(self.parts[0], slot)
                            self.send(self.parts[0], slot, self.inner, 0, way == 0)
                            self.send(self.parts[0], slot, self.inner, 1, way == 1)
                            self.seen(slot)

    def finish(self):
        @pl.loop(0, self.outer.size)
        def _(row):
            @pl.loop(0, self.inner.size)
            def _(place):
                slot = self.slot(row, place)
                for part in self.parts:
                    for way in (0, 1):
                        passed = (row <= self.outer.place) if way == 0 else (row >= self.outer.place)
                        if part[0] == 0:
                            passed &= place == self.inner.place

                        @pl.when(self.outer.has(way) & passed)
                        def _():
                            self.copy(part, slot, self.outer, way).wait_send()

                        passed = (place <= self.inner.place) if way == 0 else (place >= self.inner.place)
                        if part[0] == 1:
                            passed &= row == self.outer.place

                        @pl.when(self.inner.has(way) & passed)
                        def _():
                            self.copy(part, slot, self.inner, way).wait_send()


class Reduce:
    def __init__(self, line, term, landed, sent, recv):
        self.line, self.term, self.landed, self.sent, self.recv = line, term, landed, sent, recv

    def copy(self, way, owner):
        return pltpu.make_async_remote_copy(
            src_ref=self.term(owner),
            dst_ref=self.landed(way, owner),
            send_sem=self.sent(way, owner),
            recv_sem=self.recv(way, owner),
            device_id=self.line.next(way),
            device_id_type=MESH,
        )

    def arrive(self, way, owner):
        piece = self.landed(way, owner)
        pltpu.make_async_copy(piece, piece, self.recv(way, owner)).wait()

    def add(self, way, owner):
        @pl.when(self.line.has(1 - way))
        def _():
            self.arrive(way, owner)
            total = self.term(owner)[...].astype(WIDE) + self.landed(way, owner)[...].astype(WIDE)
            self.term(owner)[...] = total.astype(HALF)

    def step(self, distance):
        for way in (0, 1):
            owner = self.line.place + (distance if way == 0 else -distance)

            @pl.when((owner >= 0) & (owner < self.line.size))
            def _():
                self.add(way, owner)
                self.copy(way, owner).start()

    def total(self, out):
        place = self.line.place
        out[...] = self.term(place)[...].astype(out.dtype)
        for way in (0, 1):

            @pl.when(self.line.has(1 - way))
            def _():
                self.arrive(way, place)
                out[...] = (out[...].astype(WIDE) + self.landed(way, place)[...].astype(WIDE)).astype(out.dtype)

    def finish(self):
        for distance in range(1, self.line.size):
            for way in (0, 1):
                owner = self.line.place + (distance if way == 0 else -distance)

                @pl.when((owner >= 0) & (owner < self.line.size))
                def _():
                    self.copy(way, owner).wait_send()


def layer(
    sizes,
    tokens_in, wq_in, wk_in, wv_in, wo_in, cot_in, state_in,
    result, grad_tokens, grad_wq, grad_wk, grad_wv, grad_wo, grad_state,
    tok, cot, moved_tok, moved_cot, wq, wk, wv, wo, state,
    acc, grad_normed, mixed, query, keys, values, scores_t, prior,
    fore, rear, grads, normed,
    terms, terms_outer, terms_inner, summed,
    inputs, inputs_inner, inputs_outer,
    load_sem, fore_sem, rear_sem,
    tok_recv, tok_outer, tok_inner, tok_moved, tok_landed,
    cot_recv, cot_outer, cot_inner, cot_moved, cot_landed,
    grads_recv, grads_outer, grads_inner, normed_recv, normed_outer, normed_inner,
    terms_outer_sem, terms_inner_sem, inputs_inner_sem, inputs_outer_sem,
):
    seq, head, cut = sizes
    head_inner, seq_inner = inner_size(head), inner_size(seq)
    head_outer, seq_outer = head // head_inner, seq // seq_inner
    shared = head // seq
    rows, wide = tok.shape[1:]
    columns = wq.shape[1]
    heads_here = columns // DH
    s, h = lax.axis_index("seq"), lax.axis_index("head")
    z, y = h // head_inner, h % head_inner
    outer = Line(z, head_outer, lambda place: (s, place * head_inner + y))
    inner = Line(y, head_inner, lambda place: (s, z * head_inner + place))
    chip = Line(s // seq_inner, seq_outer, lambda place: (place * seq_inner + s % seq_inner, h))
    core = Line(s % seq_inner, seq_inner, lambda place: (s // seq_inner * seq_inner + place, h))

    loads = [
        pltpu.make_async_copy(source, target, load_sem.at[number])
        for number, (source, target) in enumerate(
            [
                (tokens_in, tok.at[h]),
                (wq_in, wq), (wk_in, wk), (wv_in, wv),
                (cot_in, cot.at[h]), (wo_in, wo), (state_in, state),
            ]
        )
    ]
    for load in loads:
        load.start()

    barrier = pltpu.get_barrier_semaphore()
    expected = seq - 1
    for line in (outer, inner):
        for way in (0, 1):
            expected = expected + line.has(way).astype(jnp.int32)

            @pl.when(line.has(way))
            def _():
                pl.semaphore_signal(barrier, inc=1, device_id=line.next(way), device_id_type=MESH)
    for other in range(1, seq):
        pl.semaphore_signal(barrier, inc=1, device_id=((s + other) % seq, h), device_id_type=MESH)
    pl.semaphore_wait(barrier, expected)

    def moves(slots, moved, sent, landed):
        def copy(slot):
            return pltpu.make_async_remote_copy(
                src_ref=slots.at[slot],
                dst_ref=moved.at[s, slot % shared],
                send_sem=sent.at[slot],
                recv_sem=landed.at[s, slot % shared],
                device_id=(slot // shared, h),
                device_id_type=MESH,
            )

        def start(slot):
            @pl.when(slot // shared != s)
            def _():
                copy(slot).start()

            @pl.when(slot // shared == s)
            def _():
                own = moved.at[s, slot % shared]
                pltpu.make_async_copy(slots.at[slot], own, landed.at[s, slot % shared]).start()

        def row(distance):
            @pl.loop(0, 2)
            def _(side):
                place = z + (2 * side - 1) * distance

                @pl.when((place >= 0) & (place < head_outer))
                def _():
                    for owner in range(head_inner):
                        start(place * head_inner + owner)

        def finish():
            @pl.loop(0, head)
            def _(slot):
                @pl.when(slot // shared != s)
                def _():
                    copy(slot).wait_send()

        return start, row, finish

    move_tok, move_tok_row, finish_tok = moves(tok, moved_tok, tok_moved, tok_landed)
    move_cot, move_cot_row, finish_cot = moves(cot, moved_cot, cot_moved, cot_landed)

    def project(slot):
        block = tok[slot]
        span = pl.ds(pl.multiple_of(slot * wide, wide), wide)
        for number, weight in enumerate((wq, wk, wv)):
            acc[number] += mul(block, weight[span, :])

        @pl.when((abs(slot // head_inner - z) < head_outer - 1))
        def _():
            move_tok(slot)

    def pull(slot):
        span = pl.ds(pl.multiple_of(slot * wide, wide), wide)
        grad_normed[...] += mul(cot[slot], wo[:, span], NT)
        move_cot(slot)

    tok_gather = Gather(tokens_in, tok, tok_recv, tok_outer, tok_inner, outer, inner, cut, project)
    cot_gather = Gather(cot_in, cot, cot_recv, cot_outer, cot_inner, outer, inner, cut, pull)
    nothing = lambda slot: None
    grads_gather = Gather(
        grads.at[s], grads, grads_recv, grads_outer, grads_inner, chip, core, rows, nothing
    )
    normed_gather = Gather(
        normed.at[s], normed, normed_recv, normed_outer, normed_inner, chip, core, rows, nothing
    )

    tok_gather.own(outer)
    tok_gather.own(inner)
    acc[...] = jnp.zeros_like(acc)
    grad_normed[...] = jnp.zeros_like(grad_normed)
    for load in loads[:4]:
        load.wait()
    project(h)
    tok_gather.cross_row()

    @pl.loop(1, head_outer + 1)
    def _(distance):
        pl.when(distance == head_outer - 1)(lambda: cot_gather.own(outer))
        pl.when(distance < head_outer)(lambda: tok_gather.from_outer(distance))
        pl.when(distance == head_outer - 1)(lambda: cot_gather.own(inner))
        tok_gather.from_inner(distance - 1)


    for number, target in enumerate((query, keys, values)):
        target[...] = acc[number].astype(HALF)

    def part(ref, number):
        return ref[:, number * DH : (number + 1) * DH]

    for number in range(heads_here):
        fore[s, number] = mul(part(keys, number), part(values, number), TN).astype(HALF)

    def share(states, sems, wanted):
        def copy(other):
            return pltpu.make_async_remote_copy(
                src_ref=states.at[s],
                dst_ref=states.at[s],
                send_sem=sems.at[0, other],
                recv_sem=sems.at[1, s],
                device_id=(other, h),
                device_id_type=MESH,
            )

        def start():
            for other in range(seq):
                pl.when((other != s) & wanted(s, other))(lambda: copy(other).start())

        def arrive():
            for other in range(seq):

                @pl.when((other != s) & wanted(other, s))
                def _():
                    pltpu.make_async_copy(states.at[other], states.at[other], sems.at[1, other]).wait()

        def finish():
            for other in range(seq):
                pl.when((other != s) & wanted(s, other))(lambda: copy(other).wait_send())

        return start, arrive, finish

    start_fore, arrive_fore, finish_fore = share(fore, fore_sem, lambda source, target: source < target)
    start_rear, arrive_rear, finish_rear = share(rear, rear_sem, lambda source, target: target >= 0)
    start_fore()
    for load in loads[4:]:
        load.wait()
    pull(h)
    cot_gather.cross_row()
    cot_gather.from_outer(1)
    move_tok_row(head_outer - 1)

    below = lax.broadcasted_iota(jnp.int32, (rows, rows), 1) <= lax.broadcasted_iota(jnp.int32, (rows, rows), 0)
    above = lax.broadcasted_iota(jnp.int32, (rows, rows), 1) >= lax.broadcasted_iota(jnp.int32, (rows, rows), 0)
    for number in range(heads_here):
        query_h, keys_h = part(query, number), part(keys, number)
        scores = jnp.where(below, mul(query_h, keys_h, NT), 0.0).astype(HALF)
        scores_t[number] = jnp.where(above, mul(keys_h, query_h, NT), 0.0).astype(HALF)
        mixed[:, number * DH : (number + 1) * DH] = mul(scores, part(values, number))
    arrive_fore()
    for number in range(heads_here):
        before = state[number]
        for other in range(seq):
            before = before + jnp.where(other < s, fore[other, number].astype(WIDE), 0.0)
        prior[number] = before.astype(HALF)
        whole = part(mixed, number) + mul(part(query, number), prior[number])
        mixed[:, number * DH : (number + 1) * DH] = whole
        inv_norm = lax.rsqrt(jnp.mean(whole * whole, axis=-1, keepdims=True) + EPSILON)
        normed[s, :, number * DH : (number + 1) * DH] = (whole * inv_norm).astype(HALF)
    normed_gather.own(chip)
    normed_gather.own(core)

    @pl.loop(0, head)
    def _(slot):
        span = pl.ds(pl.multiple_of(slot * wide, wide), wide)
        terms[slot // head_inner, slot % head_inner] = mul(normed[s], wo[:, span]).astype(HALF)

    outer_sums = [
        Reduce(
            outer,
            lambda owner, place=place: terms.at[owner, place],
            lambda way, owner, place=place: terms_outer.at[way, owner, place],
            lambda way, owner, place=place: terms_outer_sem.at[0, way, owner, place],
            lambda way, owner, place=place: terms_outer_sem.at[1, way, owner, place],
        )
        for place in range(head_inner)
    ]
    inner_sum = Reduce(
        inner,
        lambda owner: summed.at[owner],
        lambda way, owner: terms_inner.at[way, owner],
        lambda way, owner: terms_inner_sem.at[0, way, owner],
        lambda way, owner: terms_inner_sem.at[1, way, owner],
    )

    def result_step(distance):
        for one in outer_sums:
            one.step(distance)

    result_step(head_outer - 1)
    cot_gather.from_inner(0)
    for distance in range(2, head_outer):
        cot_gather.from_outer(distance)
        cot_gather.from_inner(distance - 1)
    for distance in range(head_outer - 2, 1, -1):
        result_step(distance)
    cot_gather.from_inner(head_outer - 1)

    for number in range(heads_here):
        whole, pulled = part(mixed, number), part(grad_normed, number)
        inv_norm = lax.rsqrt(jnp.mean(whole * whole, axis=-1, keepdims=True) + EPSILON)
        slope = jnp.mean(pulled * whole, axis=-1, keepdims=True)
        grad_mixed = (inv_norm * (pulled - whole * inv_norm * inv_norm * slope)).astype(HALF)
        grads[s, :, number * DH : (number + 1) * DH] = grad_mixed
        rear[s, number] = mul(part(query, number), grad_mixed, TN).astype(HALF)
    start_rear()
    for number in range(heads_here):
        span = slice(number * DH, (number + 1) * DH)
        grad_mixed = grads[s, :, span]
        query_h, keys_h, values_h = part(query, number), part(keys, number), part(values, number)
        grad_scores = jnp.where(below, mul(grad_mixed, values_h, NT), 0.0).astype(HALF)
        grad_scores_t = jnp.where(above, mul(values_h, grad_mixed, NT), 0.0).astype(HALF)
        acc[0, :, span] = mul(grad_scores, keys_h) + mul(grad_mixed, prior[number], NT)
        acc[1, :, span] = mul(grad_scores_t, query_h)
        acc[2, :, span] = mul(scores_t[number], grad_mixed)
    arrive_rear()
    for number in range(heads_here):
        later = jnp.zeros((DH, DH), WIDE)
        every = jnp.zeros((DH, DH), WIDE)
        for other in range(seq):
            one = rear[other, number].astype(WIDE)
            later = later + jnp.where(other > s, one, 0.0)
            every = every + one
        grad_state[number] = every
        later = later.astype(HALF)
        span = slice(number * DH, (number + 1) * DH)
        acc[1, :, span] += mul(part(values, number), later, NT)
        acc[2, :, span] += mul(part(keys, number), later)
    for number in range(3):
        grads[s, :, number * columns : (number + 1) * columns] = acc[number].astype(HALF)

    input_sums = lambda place: Reduce(
        inner,
        lambda owner: inputs.at[place, owner],
        lambda way, owner: inputs_inner.at[way, place, owner],
        lambda way, owner: inputs_inner_sem.at[0, way, place, owner],
        lambda way, owner: inputs_inner_sem.at[1, way, place, owner],
    )
    input_sum = Reduce(
        outer,
        lambda owner: inputs.at[owner, y],
        lambda way, owner: inputs_outer.at[way, owner],
        lambda way, owner: inputs_outer_sem.at[0, way, owner],
        lambda way, owner: inputs_outer_sem.at[1, way, owner],
    )

    def each_row(distance, act):
        @pl.loop(0, 2)
        def _(side):
            place = z + (2 * side - 1) * distance
            pl.when((place >= 0) & (place < head_outer) & ((distance > 0) | (side == 0)))(lambda: act(place))

    def input_terms(place):
        @pl.loop(0, head_inner)
        def _(turn):
            owner = (y + 1 + turn) % head_inner
            span = pl.ds(pl.multiple_of((place * head_inner + owner) * wide, wide), wide)
            term = mul(grads[s, :, :columns], wq[span, :], NT)
            term += mul(grads[s, :, columns : 2 * columns], wk[span, :], NT)
            term += mul(grads[s, :, 2 * columns :], wv[span, :], NT)
            inputs[place, owner] = term.astype(HALF)

        sums = input_sums(place)
        for distance in range(head_inner - 1, 0, -1):
            sums.step(distance)

    def input_inner_total(place):
        sums = input_sums(place)
        for way in (0, 1):
            sums.add(way, y)

    def input_step(distance):
        each_row(distance, input_inner_total)
        if distance:
            input_sum.step(distance)

    @pl.loop(0, head_outer)
    def _(turn):
        each_row(head_outer - 1 - turn, input_terms)
    grads_gather.own(chip)
    grads_gather.own(core)

    def weight_grads(place):
        for number in range(shared):
            piece, block = moved_tok.at[place, number], moved_cot.at[place, number]
            span = slice(number * wide, (number + 1) * wide)
            pltpu.make_async_copy(piece, piece, tok_landed.at[place, number]).wait()
            pltpu.make_async_copy(block, block, cot_landed.at[place, number]).wait()
            for target, start in ((grad_wq, 0), (grad_wk, columns), (grad_wv, 2 * columns)):
                target[span, :] += mul(piece[...], grads[place, :, start : start + columns], TN)
            grad_wo[:, span] += mul(normed[place], block[...], TN)

    for target in (grad_wq, grad_wk, grad_wv, grad_wo):
        target[...] = jnp.zeros_like(target)
    if head_outer > 2:
        result_step(1)
    normed_gather.from_outer(1)
    normed_gather.from_inner(0)
    for distance in range(2, seq_outer):
        normed_gather.from_outer(distance)
        normed_gather.from_inner(distance - 1)
    normed_gather.from_inner(seq_outer - 1)
    weight_grads(s)
    input_step(head_outer - 1)
    for place, one in enumerate(outer_sums):
        one.total(summed.at[place])
    for distance in range(head_inner - 1, 0, -1):
        inner_sum.step(distance)
    grads_gather.from_outer(1)
    grads_gather.from_inner(0)
    for distance in range(2, seq_outer):
        grads_gather.from_outer(distance)
        grads_gather.from_inner(distance - 1)
    for distance in range(head_outer - 2, 0, -1):
        input_step(distance)
    grads_gather.from_inner(seq_outer - 1)

    @pl.loop(1, seq)
    def _(other):
        weight_grads((s + other) % seq)

    inner_sum.total(result)
    input_step(0)
    input_sum.total(grad_tokens)

    for one in (tok_gather, cot_gather, grads_gather, normed_gather, *outer_sums, inner_sum, input_sum):
        one.finish()
    pl.loop(0, head_outer)(lambda place: input_sums(place).finish())
    for finish in (finish_tok, finish_cot, finish_fore, finish_rear):
        finish()


def solution(mesh):
    seq, head = mesh.shape["seq"], mesh.shape["head"]

    def on_device(tokens, w_query, w_key, w_value, w_out, grad_out, state_in):
        rows, wide = tokens.shape
        depth, columns = w_query.shape
        heads_here = columns // DH
        shared = head // seq
        assert rows == BLOCK and head % seq == 0
        head_inner, seq_inner = inner_size(head), inner_size(seq)
        head_outer, seq_outer = head // head_inner, seq // seq_inner
        cut = rows
        vmem = lambda *shape: pltpu.VMEM(shape, HALF)
        full = lambda *shape: pltpu.VMEM(shape, WIDE)
        dma = lambda *shape: pltpu.SemaphoreType.DMA(shape)
        gathers = lambda: [dma(2, head), dma(2, head, 2), dma(2, head, 2), dma(head), dma(seq, shared)]
        spans = lambda: [dma(1, seq), dma(1, seq, 2), dma(1, seq, 2)]
        outs = [
            ((rows, wide), HALF), ((rows, wide), WIDE),
            ((shared * wide, columns), WIDE), ((shared * wide, columns), WIDE), ((shared * wide, columns), WIDE),
            ((columns, shared * wide), WIDE), ((heads_here, DH, DH), WIDE),
        ]
        return pl.pallas_call(
            lambda *refs: layer((seq, head, cut), *refs),
            out_shape=[jax.ShapeDtypeStruct(shape, kind) for shape, kind in outs],
            in_specs=[pl.BlockSpec(memory_space=pl.ANY)] * 7,
            out_specs=[pl.BlockSpec(memory_space=pltpu.VMEM)] * 7,
            scratch_shapes=[
                vmem(head, rows, wide), vmem(head, rows, wide),
                vmem(seq, shared, rows, wide), vmem(seq, shared, rows, wide),
                vmem(depth, columns), vmem(depth, columns), vmem(depth, columns), vmem(columns, depth),
                full(heads_here, DH, DH),
                full(3, rows, columns), full(rows, columns), full(rows, columns),
                vmem(rows, columns), vmem(rows, columns), vmem(rows, columns),
                vmem(heads_here, rows, rows), vmem(heads_here, DH, DH),
                vmem(seq, heads_here, DH, DH), vmem(seq, heads_here, DH, DH),
                vmem(seq, rows, 3 * columns), vmem(seq, rows, columns),
                vmem(head_outer, head_inner, rows, wide), vmem(2, head_outer, head_inner, rows, wide),
                vmem(2, head_inner, rows, wide), vmem(head_inner, rows, wide),
                vmem(head_outer, head_inner, rows, wide), vmem(2, head_outer, head_inner, rows, wide),
                vmem(2, head_outer, rows, wide),
                dma(7), dma(2, seq), dma(2, seq),
                *gathers(), *gathers(), *spans(), *spans(),
                dma(2, 2, head_outer, head_inner), dma(2, 2, head_inner),
                dma(2, 2, head_outer, head_inner), dma(2, 2, head_outer),
            ],
            compiler_params=pltpu.CompilerParams(
                collective_id=0, has_side_effects=True, vmem_limit_bytes=52 * 1024 * 1024
            ),
        )(tokens, w_query, w_key, w_value, w_out, grad_out, state_in)

    by_head = P(None, "head")
    tiled = P("seq", "head")
    return jax.shard_map(
        on_device,
        mesh=mesh,
        in_specs=(tiled, by_head, by_head, by_head, P("head", None), tiled, P("head", None, None)),
        out_specs=(tiled, tiled, tiled, tiled, tiled, P("head", "seq"), P("head", None, None)),
        check_vma=False,
    )
```

profile of v0, /device:TPU:10, one launch (start us, length us, event | category | flops | bytes accessed | tf_op | source)
XLA Modules:
  0.0 131.8 jit_solution(6048713028050222901)
XLA Ops:
  0.6 0.0 copy-start
  0.6 0.9 copy-done
  1.6 0.0 copy-start.1
  1.6 0.9 copy-done.1
  2.5 0.0 copy-start.2
  2.5 0.9 copy-done.2
  3.4 120.9 %shard_map.126 = (bf16[256,512]{1,0:T(8,128)(2,1)S(1)}, f32[256,512]{1,0:T(8,128)S(1)}, f32[1024,256]{1,0:T(8,128)}, f32[1024,256]{1,0:T(8,128)}, f32[1024,256]{...) custom-call(bf16[256,512]{1,0:T(8,128)(2,1)S(1)} %copy-done, bf16[4096,256]{1,0:T(8,128)(2,1)} %refs_1_.1, ...), custom_call_target="tpu_custom_call" | custom-call | tf_op jit(solution)/shard_map/pallas_call | solution.py:614
  124.3 0.0 copy-start.5
  124.3 0.7 copy.21
  125.0 0.8 copy.22
  125.8 0.0 copy-start.4
  125.8 2.4 %copy.23 = f32[1024,256]{1,0:T(8,128)} copy(f32[1024,256]{1,0:T(8,128)} %get-tuple-element.16) | data formatting | bytes 2097152
  128.2 0.0 copy-done.5
  128.2 0.0 copy-start.3
  128.2 1.0 copy.24
  129.2 0.0 copy-done.4
  129.2 1.0 copy.25
  130.1 0.0 copy-done.3
  130.1 1.0 copy.26
  131.1 0.7 copy.27
Async XLA Ops:
  0.6 1.0 copy-start
  1.6 0.9 copy-start.1
  2.5 0.9 copy-start.2
  124.3 3.9 %copy-start.5 = (f32[1024,256]{1,0:T(8,128)S(1)}, f32[1024,256]{1,0:T(8,128)}, u32[]{:S(2)}) copy-start(f32[1024,256]{1,0:T(8,128)} %get-tuple-element.17) | copy-start | bytes 3145732
  125.8 3.3 %copy-start.4 = (f32[1024,256]{1,0:T(8,128)S(1)}, f32[1024,256]{1,0:T(8,128)}, u32[]{:S(2)}) copy-start(f32[1024,256]{1,0:T(8,128)} %get-tuple-element.18) | copy-start | bytes 3145732
  128.2 1.9 %copy-start.3 = (f32[256,1024]{1,0:T(8,128)S(1)}, f32[256,1024]{1,0:T(8,128)}, u32[]{:S(2)}) copy-start(f32[256,1024]{1,0:T(8,128)} %get-tuple-element.19) | copy-start | bytes 3145732
where the time goes:
time: 132 us
  Pallas kernels  121 us (92%)
  local copies, waits for them, and re-layouts  10.2 us (8%)
    pallas_call x1, Pallas kernels, on_device(): pl.pallas_call(lambda *refs: layer((seq, head, cut), *refs), out_shape=[j...  121 us
    unnamed x19, local copies, waits for them, and re-layouts  10.2 us

commit v1 on v0

--- a/solution.py
+++ b/solution.py
@@ -20,6 +20,26 @@
     return lax.dot_general(left, right, dims, preferred_element_type=WIDE)
 
 
+def parts(rows, shares):
+    unit, start, cut = rows // 16, 0, []
+    for order, share in shares:
+        cut.append((order, start, share * unit))
+        start += share * unit
+    return cut
+
+
+def gather_parts(rows):
+    return parts(rows, ((0, 7), (0, 6), (1, 3)))
+
+
+def result_parts(rows):
+    return parts(rows, ((1, 10), (0, 6)))
+
+
+def input_parts(rows):
+    return parts(rows, ((0, 8), (0, 8)))
+
+
 def inner_size(count):
     inner = 1
     while 4 * inner * inner <= count:
@@ -39,18 +59,17 @@
 
 
 class Gather:
-    def __init__(self, source, slots, recv, sent_outer, sent_inner, outer, inner, cut, seen):
+    def __init__(self, source, slots, recv, sent_outer, sent_inner, outer, inner, parts, seen):
         self.source, self.slots, self.recv = source, slots, recv
         self.sent_outer, self.sent_inner = sent_outer, sent_inner
         self.outer, self.inner, self.seen = outer, inner, seen
-        rows = slots.shape[1]
-        self.parts = [part for part in ((0, 0, cut), (1, cut, rows - cut)) if part[2]]
+        self.parts = [(number, *part) for number, part in enumerate(parts)]
 
     def slot(self, place_outer, place_inner):
         return place_outer * self.inner.size + place_inner
 
     def copy(self, part, slot, line, way, source=None):
-        number, start, rows = part
+        number, _, start, rows = part
         sent = self.sent_outer if line is self.outer else self.sent_inner
         piece = self.slots.at[slot, pl.ds(start, rows)]
         return pltpu.make_async_remote_copy(
@@ -68,70 +87,77 @@
             self.copy(part, slot, line, way, source).start()
 
     def arrive(self, part, slot):
-        number, start, rows = part
+        number, _, start, rows = part
         piece = self.slots.at[slot, pl.ds(start, rows)]
         pltpu.make_async_copy(piece, piece, self.recv.at[number, slot]).wait()
 
-    def own(self, line):
+    def own(self, line, orders=(0, 1)):
         slot = self.slot(self.outer.place, self.inner.place)
         for part in self.parts:
-            for way in (0, 1):
-                self.send(part, slot, line, way, source=self.source)
+            if part[1] in orders:
+                for way in (0, 1):
+                    self.send(part, slot, line, way, source=self.source)
 
     def cross_row(self):
-        for part in self.parts[1:]:
-            for way in (0, 1):
-                for step in range(1, self.inner.size):
-                    place = self.inner.place + (-step if way == 0 else step)
-
-                    @pl.when((place >= 0) & (place < self.inner.size))
-                    def _():
-                        slot = self.slot(self.outer.place, place)
-                        self.arrive(part, slot)
-                        self.send(part, slot, self.inner, way)
-                        self.send(part, slot, self.outer, 0)
-                        self.send(part, slot, self.outer, 1)
-
-    def from_outer(self, distance):
-        @pl.loop(0, 2)
-        def _(side):
-            place = self.outer.place + (2 * side - 1) * distance
-
-            @pl.when((place >= 0) & (place < self.outer.size))
-            def _():
-                mine = self.slot(place, self.inner.place)
-                for part in self.parts:
-                    owners = [self.inner.place] if part[0] == 0 else range(self.inner.size)
-                    for owner in owners:
-                        slot = self.slot(place, owner)
-                        self.arrive(part, slot)
-                        self.send(part, slot, self.outer, 0, side == 0)
-                        self.send(part, slot, self.outer, 1, side == 1)
-                    if part[0] == 0:
-                        self.send(part, mine, self.inner, 0)
-                        self.send(part, mine, self.inner, 1)
-                self.seen(mine)
-
-    def from_inner(self, distance):
+        for part in self.parts:
+            if part[1] == 1:
+                for way in (0, 1):
+                    for step in range(1, self.inner.size):
+                        place = self.inner.place + (-step if way == 0 else step)
+
+                        @pl.when((place >= 0) & (place < self.inner.size))
+                        def _():
+                            slot = self.slot(self.outer.place, place)
+                            self.arrive(part, slot)
+                            self.send(part, slot, self.inner, way)
+                            self.send(part, slot, self.outer, 0)
+                            self.send(part, slot, self.outer, 1)
+
+    def each_side(self, distance, act):
         @pl.loop(0, 2)
         def _(side):
             row = self.outer.place + (2 * side - 1) * distance
 
             @pl.when((row >= 0) & (row < self.outer.size) & ((distance > 0) | (side == 0)))
             def _():
-                @pl.loop(0, 2)
-                def _(way):
-                    @pl.loop(1, self.inner.size)
-                    def _(step):
-                        place = self.inner.place + (2 * way - 1) * step
-
-                        @pl.when((place >= 0) & (place < self.inner.size))
-                        def _():
-                            slot = self.slot(row, place)
-                            self.arrive(self.parts[0], slot)
-                            self.send(self.parts[0], slot, self.inner, 0, way == 0)
-                            self.send(self.parts[0], slot, self.inner, 1, way == 1)
-                            self.seen(slot)
+                act(side, row)
+
+    def from_outer(self, distance):
+        steps = [(part, 0) for part in self.parts]
+        steps += [(part, turn) for turn in range(1, self.inner.size) for part in self.parts if part[1] == 1]
+        for part, turn in steps:
+
+            def pass_on(side, row):
+                slot = self.slot(row, (self.inner.place + turn) % self.inner.size)
+                self.arrive(part, slot)
+                self.send(part, slot, self.outer, 0, side == 0)
+                self.send(part, slot, self.outer, 1, side == 1)
+                if part[1] == 0:
+                    self.send(part, slot, self.inner, 0)
+                    self.send(part, slot, self.inner, 1)
+
+            self.each_side(distance, pass_on)
+        self.each_side(distance, lambda side, row: self.seen(self.slot(row, self.inner.place)))
+
+    def from_inner(self, distance):
+        def each_place(side, row):
+            @pl.loop(0, 2)
+            def _(way):
+                @pl.loop(1, self.inner.size)
+                def _(step):
+                    place = self.inner.place + (2 * way - 1) * step
+
+                    @pl.when((place >= 0) & (place < self.inner.size))
+                    def _():
+                        slot = self.slot(row, place)
+                        for part in self.parts:
+                            if part[1] == 0:
+                                self.arrive(part, slot)
+                                self.send(part, slot, self.inner, 0, way == 0)
+                                self.send(part, slot, self.inner, 1, way == 1)
+                        self.seen(slot)
+
+        self.each_side(distance, each_place)
 
     def finish(self):
         @pl.loop(0, self.outer.size)
@@ -142,7 +168,7 @@
                 for part in self.parts:
                     for way in (0, 1):
                         passed = (row <= self.outer.place) if way == 0 else (row >= self.outer.place)
-                        if part[0] == 0:
+                        if part[1] == 0:
                             passed &= place == self.inner.place
 
                         @pl.when(self.outer.has(way) & passed)
@@ -150,7 +176,7 @@
                             self.copy(part, slot, self.outer, way).wait_send()
 
                         passed = (place <= self.inner.place) if way == 0 else (place >= self.inner.place)
-                        if part[0] == 1:
+                        if part[1] == 1:
                             passed &= row == self.outer.place
 
                         @pl.when(self.inner.has(way) & passed)
@@ -159,57 +185,138 @@
 
 
 class Reduce:
-    def __init__(self, line, term, landed, sent, recv):
-        self.line, self.term, self.landed, self.sent, self.recv = line, term, landed, sent, recv
+    def __init__(self, line, term, landed, sems):
+        self.line, self.term, self.landed, self.sems = line, term, landed, sems
 
     def copy(self, way, owner):
         return pltpu.make_async_remote_copy(
             src_ref=self.term(owner),
             dst_ref=self.landed(way, owner),
-            send_sem=self.sent(way, owner),
-            recv_sem=self.recv(way, owner),
+            send_sem=self.sems(0, way, owner),
+            recv_sem=self.sems(1, way, owner),
             device_id=self.line.next(way),
             device_id_type=MESH,
         )
 
-    def arrive(self, way, owner):
-        piece = self.landed(way, owner)
-        pltpu.make_async_copy(piece, piece, self.recv(way, owner)).wait()
-
-    def add(self, way, owner):
+    def arrive(self, way, owner, act):
         @pl.when(self.line.has(1 - way))
         def _():
-            self.arrive(way, owner)
-            total = self.term(owner)[...].astype(WIDE) + self.landed(way, owner)[...].astype(WIDE)
-            self.term(owner)[...] = total.astype(HALF)
-
-    def step(self, distance):
+            piece = self.landed(way, owner)
+            pltpu.make_async_copy(piece, piece, self.sems(1, way, owner)).wait()
+            act(piece[...].astype(WIDE))
+
+    def add(self, way, owner):
+        term = self.term(owner)
+
+        def act(value):
+            term[...] = (term[...].astype(WIDE) + value).astype(HALF)
+
+        self.arrive(way, owner, act)
+
+    def each(self, distance, act):
         for way in (0, 1):
             owner = self.line.place + (distance if way == 0 else -distance)
-
-            @pl.when((owner >= 0) & (owner < self.line.size))
-            def _():
-                self.add(way, owner)
-                self.copy(way, owner).start()
-
-    def total(self, out):
-        place = self.line.place
-        out[...] = self.term(place)[...].astype(out.dtype)
-        for way in (0, 1):
-
-            @pl.when(self.line.has(1 - way))
-            def _():
-                self.arrive(way, place)
-                out[...] = (out[...].astype(WIDE) + self.landed(way, place)[...].astype(WIDE)).astype(out.dtype)
+            pl.when((owner >= 0) & (owner < self.line.size))(lambda: act(way, owner))
+
+    def step(self, distance):
+        def act(way, owner):
+            self.add(way, owner)
+            self.copy(way, owner).start()
+
+        self.each(distance, act)
 
     def finish(self):
         for distance in range(1, self.line.size):
+            self.each(distance, lambda way, owner: self.copy(way, owner).wait_send())
+
+
+class Scatter:
+    def __init__(self, terms, landed, sems, outer, inner, parts):
+        self.terms, self.landed, self.sems = terms, landed, sems
+        self.outer, self.inner = outer, inner
+        self.parts = [(number, *part) for number, part in enumerate(parts)]
+
+    def along_outer(self, part, place):
+        number, _, start, rows = part
+        span = pl.ds(start, rows)
+        return Reduce(
+            self.outer,
+            lambda owner: self.terms.at[owner, place, span],
+            lambda way, owner: self.landed.at[0, way, owner, place, span],
+            lambda end, way, owner: self.sems.at[number, 0, end, way, owner, place],
+        )
+
+    def along_inner(self, part, row):
+        number, _, start, rows = part
+        span = pl.ds(start, rows)
+        return Reduce(
+            self.inner,
+            lambda owner: self.terms.at[row, owner, span],
+            lambda way, owner: self.landed.at[1, way, row, owner, span],
+            lambda end, way, owner: self.sems.at[number, 1, end, way, row, owner],
+        )
+
+    def steps_inner(self, part, row):
+        line = self.along_inner(part, row)
+        for distance in range(self.inner.size - 1, 0, -1):
+            line.step(distance)
+
+    def start_row(self, row):
+        for part in self.parts:
+            if part[1] == 0:
+                self.steps_inner(part, row)
+
+    def outer_first(self, distance):
+        for part in self.parts:
+            if part[1] == 1:
+                for place in range(self.inner.size):
+                    self.along_outer(part, place).step(distance)
+
+    def outer_second(self, distance):
+        for part in self.parts:
+            if part[1] == 0:
+
+                def act(way, row):
+                    for side in (0, 1):
+                        self.along_inner(part, row).add(side, self.inner.place)
+
+                self.along_outer(part, self.inner.place).each(distance, act)
+                self.along_outer(part, self.inner.place).step(distance)
+
+    def turn(self):
+        for part in self.parts:
+            if part[1] == 1:
+                for place in range(self.inner.size):
+
+                    @pl.when(place != self.inner.place)
+                    def _():
+                        for way in (0, 1):
+                            self.along_outer(part, place).add(way, self.outer.place)
+
+                self.steps_inner(part, self.outer.place)
+
+    def total(self, out):
+        row, place = self.outer.place, self.inner.place
+        for part in self.parts:
+            span = pl.ds(part[2], part[3])
+            held = [self.terms[row, place, span].astype(WIDE)]
+            out[span, :] = held[0].astype(out.dtype)
+
+            def act(value):
+                out[span, :] = (out[span, :].astype(WIDE) + value).astype(out.dtype)
+
             for way in (0, 1):
-                owner = self.line.place + (distance if way == 0 else -distance)
-
-                @pl.when((owner >= 0) & (owner < self.line.size))
-                def _():
-                    self.copy(way, owner).wait_send()
+                self.along_outer(part, place).arrive(way, row, act)
+                self.along_inner(part, row).arrive(way, place, act)
+
+    def finish(self):
+        for part in self.parts:
+            if part[1] == 0:
+                pl.loop(0, self.outer.size)(lambda row: self.along_inner(part, row).finish())
+                self.along_outer(part, self.inner.place).finish()
+            else:
+                pl.loop(0, self.inner.size)(lambda place: self.along_outer(part, place).finish())
+                self.along_inner(part, self.outer.place).finish()
 
 
 def layer(
@@ -219,15 +326,14 @@
     tok, cot, moved_tok, moved_cot, wq, wk, wv, wo, state,
     acc, grad_normed, mixed, query, keys, values, scores_t, prior,
     fore, rear, grads, normed,
-    terms, terms_outer, terms_inner, summed,
-    inputs, inputs_inner, inputs_outer,
+    terms, terms_landed, inputs, inputs_landed, total,
     load_sem, fore_sem, rear_sem,
     tok_recv, tok_outer, tok_inner, tok_moved, tok_landed,
     cot_recv, cot_outer, cot_inner, cot_moved, cot_landed,
     grads_recv, grads_outer, grads_inner, normed_recv, normed_outer, normed_inner,
-    terms_outer_sem, terms_inner_sem, inputs_inner_sem, inputs_outer_sem,
+    terms_sem, inputs_sem,
 ):
-    seq, head, cut = sizes
+    seq, head = sizes
     head_inner, seq_inner = inner_size(head), inner_size(seq)
     head_outer, seq_outer = head // head_inner, seq // seq_inner
     shared = head // seq
@@ -323,20 +429,30 @@
     def pull(slot):
         span = pl.ds(pl.multiple_of(slot * wide, wide), wide)
         grad_normed[...] += mul(cot[slot], wo[:, span], NT)
-        move_cot(slot)
-
-    tok_gather = Gather(tokens_in, tok, tok_recv, tok_outer, tok_inner, outer, inner, cut, project)
-    cot_gather = Gather(cot_in, cot, cot_recv, cot_outer, cot_inner, outer, inner, cut, pull)
+
+        @pl.when((abs(slot // head_inner - z) < head_outer - 1))
+        def _():
+            move_cot(slot)
+
+    def each_row(distance, act):
+        @pl.loop(0, 2)
+        def _(side):
+            place = z + (2 * side - 1) * distance
+            pl.when((place >= 0) & (place < head_outer) & ((distance > 0) | (side == 0)))(lambda: act(place))
+
+    tok_gather = Gather(tokens_in, tok, tok_recv, tok_outer, tok_inner, outer, inner, gather_parts(rows), project)
+    cot_gather = Gather(cot_in, cot, cot_recv, cot_outer, cot_inner, outer, inner, gather_parts(rows), pull)
     nothing = lambda slot: None
     grads_gather = Gather(
-        grads.at[s], grads, grads_recv, grads_outer, grads_inner, chip, core, rows, nothing
+        grads.at[s], grads, grads_recv, grads_outer, grads_inner, chip, core, ((0, 0, rows),), nothing
     )
     normed_gather = Gather(
-        normed.at[s], normed, normed_recv, normed_outer, normed_inner, chip, core, rows, nothing
+        normed.at[s], normed, normed_recv, normed_outer, normed_inner, chip, core, ((0, 0, rows),), nothing
     )
 
+    tok_gather.own(inner, (1,))
     tok_gather.own(outer)
-    tok_gather.own(inner)
+    tok_gather.own(inner, (0,))
     acc[...] = jnp.zeros_like(acc)
     grad_normed[...] = jnp.zeros_like(grad_normed)
     for load in loads[:4]:
@@ -344,13 +460,20 @@
     project(h)
     tok_gather.cross_row()
 
-    @pl.loop(1, head_outer + 1)
+    @pl.loop(1, head_outer)
     def _(distance):
-        pl.when(distance == head_outer - 1)(lambda: cot_gather.own(outer))
-        pl.when(distance < head_outer)(lambda: tok_gather.from_outer(distance))
-        pl.when(distance == head_outer - 1)(lambda: cot_gather.own(inner))
+        tok_gather.from_outer(distance)
+
+        @pl.when(distance == head_outer - 2)
+        def _():
+            cot_gather.own(outer)
+            cot_gather.own(inner, (1,))
+
         tok_gather.from_inner(distance - 1)
 
+    cot_gather.own(inner, (0,))
+    cot_gather.cross_row()
+    tok_gather.from_inner(head_outer - 1)
 
     for number, target in enumerate((query, keys, values)):
         target[...] = acc[number].astype(HALF)
@@ -394,10 +517,9 @@
     start_fore()
     for load in loads[4:]:
         load.wait()
+    move_tok_row(head_outer - 1)
     pull(h)
-    cot_gather.cross_row()
     cot_gather.from_outer(1)
-    move_tok_row(head_outer - 1)
 
     below = lax.broadcasted_iota(jnp.int32, (rows, rows), 1) <= lax.broadcasted_iota(jnp.int32, (rows, rows), 0)
     above = lax.broadcasted_iota(jnp.int32, (rows, rows), 1) >= lax.broadcasted_iota(jnp.int32, (rows, rows), 0)
@@ -424,35 +546,20 @@
         span = pl.ds(pl.multiple_of(slot * wide, wide), wide)
         terms[slot // head_inner, slot % head_inner] = mul(normed[s], wo[:, span]).astype(HALF)
 
-    outer_sums = [
-        Reduce(
-            outer,
-            lambda owner, place=place: terms.at[owner, place],
-            lambda way, owner, place=place: terms_outer.at[way, owner, place],
-            lambda way, owner, place=place: terms_outer_sem.at[0, way, owner, place],
-            lambda way, owner, place=place: terms_outer_sem.at[1, way, owner, place],
-        )
-        for place in range(head_inner)
-    ]
-    inner_sum = Reduce(
-        inner,
-        lambda owner: summed.at[owner],
-        lambda way, owner: terms_inner.at[way, owner],
-        lambda way, owner: terms_inner_sem.at[0, way, owner],
-        lambda way, owner: terms_inner_sem.at[1, way, owner],
-    )
-
-    def result_step(distance):
-        for one in outer_sums:
-            one.step(distance)
-
-    result_step(head_outer - 1)
+    result_sums = Scatter(terms, terms_landed, terms_sem, outer, inner, result_parts(rows))
+    result_sums.outer_first(head_outer - 1)
     cot_gather.from_inner(0)
     for distance in range(2, head_outer):
         cot_gather.from_outer(distance)
-        cot_gather.from_inner(distance - 1)
-    for distance in range(head_outer - 2, 1, -1):
-        result_step(distance)
+        if distance < head_outer - 1:
+            cot_gather.from_inner(distance - 1)
+            result_sums.outer_first(head_outer - distance)
+
+    @pl.loop(0, head_outer)
+    def _(turn):
+        each_row(head_outer - 1 - turn, result_sums.start_row)
+
+    cot_gather.from_inner(head_outer - 2)
     cot_gather.from_inner(head_outer - 1)
 
     for number in range(heads_here):
@@ -463,6 +570,11 @@
         grads[s, :, number * DH : (number + 1) * DH] = grad_mixed
         rear[s, number] = mul(part(query, number), grad_mixed, TN).astype(HALF)
     start_rear()
+    move_cot_row(head_outer - 1)
+    result_sums.outer_second(head_outer - 1)
+    tok_gather.finish()
+    finish_tok()
+    finish_fore()
     for number in range(heads_here):
         span = slice(number * DH, (number + 1) * DH)
         grad_mixed = grads[s, :, span]
@@ -488,26 +600,7 @@
     for number in range(3):
         grads[s, :, number * columns : (number + 1) * columns] = acc[number].astype(HALF)
 
-    input_sums = lambda place: Reduce(
-        inner,
-        lambda owner: inputs.at[place, owner],
-        lambda way, owner: inputs_inner.at[way, place, owner],
-        lambda way, owner: inputs_inner_sem.at[0, way, place, owner],
-        lambda way, owner: inputs_inner_sem.at[1, way, place, owner],
-    )
-    input_sum = Reduce(
-        outer,
-        lambda owner: inputs.at[owner, y],
-        lambda way, owner: inputs_outer.at[way, owner],
-        lambda way, owner: inputs_outer_sem.at[0, way, owner],
-        lambda way, owner: inputs_outer_sem.at[1, way, owner],
-    )
-
-    def each_row(distance, act):
-        @pl.loop(0, 2)
-        def _(side):
-            place = z + (2 * side - 1) * distance
-            pl.when((place >= 0) & (place < head_outer) & ((distance > 0) | (side == 0)))(lambda: act(place))
+    input_sums = Scatter(inputs, inputs_landed, inputs_sem, outer, inner, input_parts(rows))
 
     def input_terms(place):
         @pl.loop(0, head_inner)
@@ -519,25 +612,18 @@
             term += mul(grads[s, :, 2 * columns :], wv[span, :], NT)
             inputs[place, owner] = term.astype(HALF)
 
-        sums = input_sums(place)
-        for distance in range(head_inner - 1, 0, -1):
-            sums.step(distance)
-
-    def input_inner_total(place):
-        sums = input_sums(place)
-        for way in (0, 1):
-            sums.add(way, y)
-
-    def input_step(distance):
-        each_row(distance, input_inner_total)
-        if distance:
-            input_sum.step(distance)
-
-    @pl.loop(0, head_outer)
+            @pl.when(turn == head_inner - 2)
+            def _():
+                input_sums.start_row(place)
+
+    each_row(head_outer - 1, input_terms)
+    input_sums.outer_first(head_outer - 1)
+    grads_gather.own(chip)
+    grads_gather.own(core)
+
+    @pl.loop(1, head_outer)
     def _(turn):
         each_row(head_outer - 1 - turn, input_terms)
-    grads_gather.own(chip)
-    grads_gather.own(core)
 
     def weight_grads(place):
         for number in range(shared):
@@ -551,42 +637,51 @@
 
     for target in (grad_wq, grad_wk, grad_wv, grad_wo):
         target[...] = jnp.zeros_like(target)
-    if head_outer > 2:
-        result_step(1)
+    result_sums.outer_first(1)
+    input_sums.outer_second(head_outer - 1)
     normed_gather.from_outer(1)
     normed_gather.from_inner(0)
     for distance in range(2, seq_outer):
         normed_gather.from_outer(distance)
         normed_gather.from_inner(distance - 1)
     normed_gather.from_inner(seq_outer - 1)
-    weight_grads(s)
-    input_step(head_outer - 1)
-    for place, one in enumerate(outer_sums):
-        one.total(summed.at[place])
-    for distance in range(head_inner - 1, 0, -1):
-        inner_sum.step(distance)
-    grads_gather.from_outer(1)
-    grads_gather.from_inner(0)
+    for distance in range(head_outer - 2, 0, -1):
+        result_sums.outer_second(distance)
+        input_sums.outer_first(distance)
+        input_sums.outer_second(distance)
+        if distance == head_outer - 2:
+            grads_gather.from_outer(1)
+            grads_gather.from_inner(0)
     for distance in range(2, seq_outer):
         grads_gather.from_outer(distance)
         grads_gather.from_inner(distance - 1)
-    for distance in range(head_outer - 2, 0, -1):
-        input_step(distance)
+    result_sums.turn()
+    input_sums.turn()
+    weight_grads(s)
     grads_gather.from_inner(seq_outer - 1)
 
     @pl.loop(1, seq)
     def _(other):
         weight_grads((s + other) % seq)
 
-    inner_sum.total(result)
-    input_step(0)
-    input_sum.total(grad_tokens)
-
-    for one in (tok_gather, cot_gather, grads_gather, normed_gather, *outer_sums, inner_sum, input_sum):
+    cot_gather.finish()
+    finish_cot()
+    finish_rear()
+    normed_gather.finish()
+    result_sums.total(total)
+    result[...] = total[...].astype(HALF)
+    input_sums.total(grad_tokens)
+    for one in (grads_gather, result_sums, input_sums):
         one.finish()
-    pl.loop(0, head_outer)(lambda place: input_sums(place).finish())
-    for finish in (finish_tok, finish_cot, finish_fore, finish_rear):
-        finish()
+
+
+def write_out(*refs):
+    count = (len(refs) - 1) // 2
+    copies = [pltpu.make_async_copy(refs[k], refs[count + k], refs[-1].at[k]) for k in range(count)]
+    for copy in copies:
+        copy.start()
+    for copy in copies:
+        copy.wait()
 
 
 def solution(mesh):
@@ -600,21 +695,23 @@
         assert rows == BLOCK and head % seq == 0
         head_inner, seq_inner = inner_size(head), inner_size(seq)
         head_outer, seq_outer = head // head_inner, seq // seq_inner
-        cut = rows
         vmem = lambda *shape: pltpu.VMEM(shape, HALF)
         full = lambda *shape: pltpu.VMEM(shape, WIDE)
         dma = lambda *shape: pltpu.SemaphoreType.DMA(shape)
-        gathers = lambda: [dma(2, head), dma(2, head, 2), dma(2, head, 2), dma(head), dma(seq, shared)]
+        pieces = len(gather_parts(rows))
+        gathers = lambda: [
+            dma(pieces, head), dma(pieces, head, 2), dma(pieces, head, 2), dma(head), dma(seq, shared)
+        ]
         spans = lambda: [dma(1, seq), dma(1, seq, 2), dma(1, seq, 2)]
         outs = [
             ((rows, wide), HALF), ((rows, wide), WIDE),
             ((shared * wide, columns), WIDE), ((shared * wide, columns), WIDE), ((shared * wide, columns), WIDE),
             ((columns, shared * wide), WIDE), ((heads_here, DH, DH), WIDE),
         ]
-        return pl.pallas_call(
-            lambda *refs: layer((seq, head, cut), *refs),
-            out_shape=[jax.ShapeDtypeStruct(shape, kind) for shape, kind in outs],
-            in_specs=[pl.BlockSpec(memory_space=pl.ANY)] * 7,
+        done = pl.pallas_call(
+            lambda *refs: layer((seq, head), *refs),
+            out_shape=[pltpu.VMEM(shape, kind) for shape, kind in outs],
+            in_specs=[pl.BlockSpec(memory_space=pltpu.HBM)] * 7,
             out_specs=[pl.BlockSpec(memory_space=pltpu.VMEM)] * 7,
             scratch_shapes=[
                 vmem(head, rows, wide), vmem(head, rows, wide),
@@ -626,19 +723,26 @@
                 vmem(heads_here, rows, rows), vmem(heads_here, DH, DH),
                 vmem(seq, heads_here, DH, DH), vmem(seq, heads_here, DH, DH),
                 vmem(seq, rows, 3 * columns), vmem(seq, rows, columns),
-                vmem(head_outer, head_inner, rows, wide), vmem(2, head_outer, head_inner, rows, wide),
-                vmem(2, head_inner, rows, wide), vmem(head_inner, rows, wide),
-                vmem(head_outer, head_inner, rows, wide), vmem(2, head_outer, head_inner, rows, wide),
-                vmem(2, head_outer, rows, wide),
+                vmem(head_outer, head_inner, rows, wide), vmem(2, 2, head_outer, head_inner, rows, wide),
+                vmem(head_outer, head_inner, rows, wide), vmem(2, 2, head_outer, head_inner, rows, wide),
+                full(rows, wide),
                 dma(7), dma(2, seq), dma(2, seq),
                 *gathers(), *gathers(), *spans(), *spans(),
-                dma(2, 2, head_outer, head_inner), dma(2, 2, head_inner),
-                dma(2, 2, head_outer, head_inner), dma(2, 2, head_outer),
+                dma(len(result_parts(rows)), 2, 2, 2, head_outer, head_inner),
+                dma(len(input_parts(rows)), 2, 2, 2, head_outer, head_inner),
             ],
             compiler_params=pltpu.CompilerParams(
-                collective_id=0, has_side_effects=True, vmem_limit_bytes=52 * 1024 * 1024
+                collective_id=0, has_side_effects=True, vmem_limit_bytes=54 * 1024 * 1024
             ),
         )(tokens, w_query, w_key, w_value, w_out, grad_out, state_in)
+        return pl.pallas_call(
+            write_out,
+            out_shape=[jax.ShapeDtypeStruct(shape, kind) for shape, kind in outs],
+            in_specs=[pl.BlockSpec(memory_space=pl.ANY)] * 7,
+            out_specs=[pl.BlockSpec(memory_space=pltpu.HBM)] * 7,
+            scratch_shapes=[dma(7)],
+            compiler_params=pltpu.CompilerParams(vmem_limit_bytes=1024 * 1024),
+        )(*done)
 
     by_head = P(None, "head")
     tiled = P("seq", "head")

time: 132 us -> 106 us (0.80)
  Pallas kernels: 121 us -> 105 us
  local copies, waits for them, and re-layouts: 10.2 us -> 0 us
    pallas_call x1 -> x2, Pallas kernels: 121 us -> 105 us  [the longest x1 103 us: on_device(): pl.pallas_call(lambda *refs: layer((seq, head), *refs), out_shape=[pltpu....]
    unnamed x19 -> x0, local copies, waits for them, and re-layouts: 10.2 us -> none
where the time goes in v1:
time: 106 us
  Pallas kernels  105 us (99%)
    pallas_call x1, Pallas kernels, on_device(): pl.pallas_call(lambda *refs: layer((seq, head), *refs), out_shape=[pltpu....  103 us
    pallas_call x1, Pallas kernels, on_device(): pl.pallas_call(write_out, out_shape=[jax.ShapeDtypeStruct(shape, kind) fo...  2.36 us

profile of v1, /device:TPU:10, one launch (start us, length us, event | category | flops | bytes accessed | tf_op | source)
XLA Modules:
  0.0 105.7 jit_solution(10876037272446372052)
XLA Ops:
  0.6 102.5 %shard_map.126 = (bf16[256,512]{1,0:T(8,128)(2,1)S(1)}, f32[256,512]{1,0:T(8,128)S(1)}, f32[1024,256]{1,0:T(8,128)S(1)}, f32[1024,256]{1,0:T(8,128)S(1)}, f32[10...) custom-call(bf16[256,512]{1,0:T(8,128)(2,1)} %refs_0_.1, bf16[4096,256]{1,0:T(8,128)(2,1)} %refs_1_.1, ...), custom_call_target="tpu_custom_call" | custom-call | tf_op jit(solution)/shard_map/pallas_call | solution.py:711
  103.2 2.4 %shard_map.127 = (bf16[256,512]{1,0:T(8,128)(2,1)}, f32[256,512]{1,0:T(8,128)}, f32[1024,256]{1,0:T(8,128)}, f32[1024,256]{1,0:T(8,128)}, f32[1024,256]{1,0:T(8,...) custom-call(bf16[256,512]{1,0:T(8,128)(2,1)S(1)} %get-tuple-element.14.refs_0_, ...), custom_call_target="tpu_custom_call" | custom-call | tf_op jit(solution)/shard_map/pallas_call | solution.py:738

commit v2 on v1

--- a/solution.py
+++ b/solution.py
@@ -37,7 +37,7 @@
 
 
 def input_parts(rows):
-    return parts(rows, ((0, 8), (0, 8)))
+    return parts(rows, ((0, 7), (0, 7), (1, 2)))
 
 
 def inner_size(count):
@@ -323,15 +323,15 @@
     sizes,
     tokens_in, wq_in, wk_in, wv_in, wo_in, cot_in, state_in,
     result, grad_tokens, grad_wq, grad_wk, grad_wv, grad_wo, grad_state,
-    tok, cot, moved_tok, moved_cot, wq, wk, wv, wo, state,
+    tok, cot, moved_tok, wq, wk, wv, wo, state,
     acc, grad_normed, mixed, query, keys, values, scores_t, prior,
     fore, rear, grads, normed,
-    terms, terms_landed, inputs, inputs_landed, total,
+    terms, terms_landed, inputs, inputs_landed, outers, outers_landed, total, total_wo,
     load_sem, fore_sem, rear_sem,
     tok_recv, tok_outer, tok_inner, tok_moved, tok_landed,
-    cot_recv, cot_outer, cot_inner, cot_moved, cot_landed,
-    grads_recv, grads_outer, grads_inner, normed_recv, normed_outer, normed_inner,
-    terms_sem, inputs_sem,
+    cot_recv, cot_outer, cot_inner,
+    grads_recv, grads_outer, grads_inner,
+    terms_sem, inputs_sem, outers_sem,
 ):
     seq, head = sizes
     head_inner, seq_inner = inner_size(head), inner_size(seq)
@@ -373,6 +373,12 @@
         pl.semaphore_signal(barrier, inc=1, device_id=((s + other) % seq, h), device_id_type=MESH)
     pl.semaphore_wait(barrier, expected)
 
+    def early(slot):
+        distance = abs(slot // head_inner - z)
+        at_end = (z == 0) | (z == head_outer - 1)
+        direct = (slot % head_inner == y) & at_end
+        return (distance < head_outer - 2) | ((distance == head_outer - 2) & direct)
+
     def moves(slots, moved, sent, landed):
         def copy(slot):
             return pltpu.make_async_remote_copy(
@@ -394,15 +400,13 @@
                 own = moved.at[s, slot % shared]
                 pltpu.make_async_copy(slots.at[slot], own, landed.at[s, slot % shared]).start()
 
-        def row(distance):
-            @pl.loop(0, 2)
-            def _(side):
-                place = z + (2 * side - 1) * distance
-
-                @pl.when((place >= 0) & (place < head_outer))
-                def _():
-                    for owner in range(head_inner):
-                        start(place * head_inner + owner)
+        def soon(slot):
+            pl.when(early(slot))(lambda: start(slot))
+
+        def late():
+            @pl.loop(0, head)
+            def _(slot):
+                pl.when(jnp.logical_not(early(slot)))(lambda: start(slot))
 
         def finish():
             @pl.loop(0, head)
@@ -411,28 +415,20 @@
                 def _():
                     copy(slot).wait_send()
 
-        return start, row, finish
-
-    move_tok, move_tok_row, finish_tok = moves(tok, moved_tok, tok_moved, tok_landed)
-    move_cot, move_cot_row, finish_cot = moves(cot, moved_cot, cot_moved, cot_landed)
+        return soon, late, finish
+
+    move_tok, move_tok_late, finish_tok = moves(tok, moved_tok, tok_moved, tok_landed)
 
     def project(slot):
         block = tok[slot]
         span = pl.ds(pl.multiple_of(slot * wide, wide), wide)
         for number, weight in enumerate((wq, wk, wv)):
             acc[number] += mul(block, weight[span, :])
-
-        @pl.when((abs(slot // head_inner - z) < head_outer - 1))
-        def _():
-            move_tok(slot)
+        move_tok(slot)
 
     def pull(slot):
         span = pl.ds(pl.multiple_of(slot * wide, wide), wide)
         grad_normed[...] += mul(cot[slot], wo[:, span], NT)
-
-        @pl.when((abs(slot // head_inner - z) < head_outer - 1))
-        def _():
-            move_cot(slot)
 
     def each_row(distance, act):
         @pl.loop(0, 2)
@@ -445,9 +441,6 @@
     nothing = lambda slot: None
     grads_gather = Gather(
         grads.at[s], grads, grads_recv, grads_outer, grads_inner, chip, core, ((0, 0, rows),), nothing
-    )
-    normed_gather = Gather(
-        normed.at[s], normed, normed_recv, normed_outer, normed_inner, chip, core, ((0, 0, rows),), nothing
     )
 
     tok_gather.own(inner, (1,))
@@ -517,7 +510,7 @@
     start_fore()
     for load in loads[4:]:
         load.wait()
-    move_tok_row(head_outer - 1)
+    move_tok_late()
     pull(h)
     cot_gather.from_outer(1)
 
@@ -537,14 +530,12 @@
         whole = part(mixed, number) + mul(part(query, number), prior[number])
         mixed[:, number * DH : (number + 1) * DH] = whole
         inv_norm = lax.rsqrt(jnp.mean(whole * whole, axis=-1, keepdims=True) + EPSILON)
-        normed[s, :, number * DH : (number + 1) * DH] = (whole * inv_norm).astype(HALF)
-    normed_gather.own(chip)
-    normed_gather.own(core)
+        normed[:, number * DH : (number + 1) * DH] = (whole * inv_norm).astype(HALF)
 
     @pl.loop(0, head)
     def _(slot):
         span = pl.ds(pl.multiple_of(slot * wide, wide), wide)
-        terms[slot // head_inner, slot % head_inner] = mul(normed[s], wo[:, span]).astype(HALF)
+        terms[slot // head_inner, slot % head_inner] = mul(normed[...], wo[:, span]).astype(HALF)
 
     result_sums = Scatter(terms, terms_landed, terms_sem, outer, inner, result_parts(rows))
     result_sums.outer_first(head_outer - 1)
@@ -570,11 +561,17 @@
         grads[s, :, number * DH : (number + 1) * DH] = grad_mixed
         rear[s, number] = mul(part(query, number), grad_mixed, TN).astype(HALF)
     start_rear()
-    move_cot_row(head_outer - 1)
-    result_sums.outer_second(head_outer - 1)
-    tok_gather.finish()
-    finish_tok()
-    finish_fore()
+
+    outer_grads = Scatter(outers, outers_landed, outers_sem, chip, core, ((0, 0, shared * columns),))
+
+    @pl.loop(0, head)
+    def _(slot):
+        owner = slot // shared
+        span = pl.ds(pl.multiple_of(slot % shared * columns, columns), columns)
+        share_wo = mul(normed[...], cot[slot], TN).astype(HALF)
+        outers[owner // seq_inner, owner % seq_inner, span] = share_wo
+
+    pl.loop(0, seq_outer)(outer_grads.start_row)
     for number in range(heads_here):
         span = slice(number * DH, (number + 1) * DH)
         grad_mixed = grads[s, :, span]
@@ -584,6 +581,11 @@
         acc[0, :, span] = mul(grad_scores, keys_h) + mul(grad_mixed, prior[number], NT)
         acc[1, :, span] = mul(grad_scores_t, query_h)
         acc[2, :, span] = mul(scores_t[number], grad_mixed)
+    result_sums.outer_second(head_outer - 1)
+    tok_gather.finish()
+    finish_tok()
+    finish_fore()
+    result_sums.outer_first(1)
     arrive_rear()
     for number in range(heads_here):
         later = jnp.zeros((DH, DH), WIDE)
@@ -627,24 +629,17 @@
 
     def weight_grads(place):
         for number in range(shared):
-            piece, block = moved_tok.at[place, number], moved_cot.at[place, number]
+            piece = moved_tok.at[place, number]
             span = slice(number * wide, (number + 1) * wide)
             pltpu.make_async_copy(piece, piece, tok_landed.at[place, number]).wait()
-            pltpu.make_async_copy(block, block, cot_landed.at[place, number]).wait()
             for target, start in ((grad_wq, 0), (grad_wk, columns), (grad_wv, 2 * columns)):
                 target[span, :] += mul(piece[...], grads[place, :, start : start + columns], TN)
-            grad_wo[:, span] += mul(normed[place], block[...], TN)
-
-    for target in (grad_wq, grad_wk, grad_wv, grad_wo):
+
+    for target in (grad_wq, grad_wk, grad_wv):
         target[...] = jnp.zeros_like(target)
-    result_sums.outer_first(1)
+    for distance in range(seq_outer - 1, 0, -1):
+        outer_grads.outer_second(distance)
     input_sums.outer_second(head_outer - 1)
-    normed_gather.from_outer(1)
-    normed_gather.from_inner(0)
-    for distance in range(2, seq_outer):
-        normed_gather.from_outer(distance)
-        normed_gather.from_inner(distance - 1)
-    normed_gather.from_inner(seq_outer - 1)
     for distance in range(head_outer - 2, 0, -1):
         result_sums.outer_second(distance)
         input_sums.outer_first(distance)
@@ -664,10 +659,12 @@
     def _(other):
         weight_grads((s + other) % seq)
 
+    outer_grads.total(total_wo)
+    for number in range(shared):
+        grad_wo[:, number * wide : (number + 1) * wide] = total_wo[number * columns : (number + 1) * columns, :]
     cot_gather.finish()
-    finish_cot()
     finish_rear()
-    normed_gather.finish()
+    outer_grads.finish()
     result_sums.total(total)
     result[...] = total[...].astype(HALF)
     input_sums.total(grad_tokens)
@@ -700,7 +697,7 @@
         dma = lambda *shape: pltpu.SemaphoreType.DMA(shape)
         pieces = len(gather_parts(rows))
         gathers = lambda: [
-            dma(pieces, head), dma(pieces, head, 2), dma(pieces, head, 2), dma(head), dma(seq, shared)
+            dma(pieces, head), dma(pieces, head, 2), dma(pieces, head, 2)
         ]
         spans = lambda: [dma(1, seq), dma(1, seq, 2), dma(1, seq, 2)]
         outs = [
@@ -715,21 +712,24 @@
             out_specs=[pl.BlockSpec(memory_space=pltpu.VMEM)] * 7,
             scratch_shapes=[
                 vmem(head, rows, wide), vmem(head, rows, wide),
-                vmem(seq, shared, rows, wide), vmem(seq, shared, rows, wide),
+                vmem(seq, shared, rows, wide),
                 vmem(depth, columns), vmem(depth, columns), vmem(depth, columns), vmem(columns, depth),
                 full(heads_here, DH, DH),
                 full(3, rows, columns), full(rows, columns), full(rows, columns),
                 vmem(rows, columns), vmem(rows, columns), vmem(rows, columns),
                 vmem(heads_here, rows, rows), vmem(heads_here, DH, DH),
                 vmem(seq, heads_here, DH, DH), vmem(seq, heads_here, DH, DH),
-                vmem(seq, rows, 3 * columns), vmem(seq, rows, columns),
+                vmem(seq, rows, 3 * columns), vmem(rows, columns),
                 vmem(head_outer, head_inner, rows, wide), vmem(2, 2, head_outer, head_inner, rows, wide),
                 vmem(head_outer, head_inner, rows, wide), vmem(2, 2, head_outer, head_inner, rows, wide),
-                full(rows, wide),
+                vmem(seq_outer, seq_inner, shared * columns, wide),
+                vmem(2, 2, seq_outer, seq_inner, shared * columns, wide),
+                full(rows, wide), full(shared * columns, wide),
                 dma(7), dma(2, seq), dma(2, seq),
-                *gathers(), *gathers(), *spans(), *spans(),
+                *gathers(), dma(head), dma(seq, shared), *gathers(), *spans(),
                 dma(len(result_parts(rows)), 2, 2, 2, head_outer, head_inner),
                 dma(len(input_parts(rows)), 2, 2, 2, head_outer, head_inner),
+                dma(1, 2, 2, 2, seq_outer, seq_inner),
             ],
             compiler_params=pltpu.CompilerParams(
                 collective_id=0, has_side_effects=True, vmem_limit_bytes=54 * 1024 * 1024

time: 106 us -> 95.2 us (0.90)
  Pallas kernels: 105 us -> 93.9 us
    pallas_call x1, Pallas kernels: 103 us -> 91.5 us  [on_device(): pl.pallas_call(lambda *refs: layer((seq, head), *refs), out_shape=[pltpu....]
where the time goes in v2:
time: 95.2 us; the launch traced here: 94.7 us
  Pallas kernels  93.9 us (99%)
    pallas_call x1, Pallas kernels, on_device(): pl.pallas_call(lambda *refs: layer((seq, head), *refs), out_shape=[pltpu....  91.5 us
    pallas_call x1, Pallas kernels, on_device(): pl.pallas_call(write_out, out_shape=[jax.ShapeDtypeStruct(shape, kind) fo...  2.36 us

profile of v2, /device:TPU:10, one launch (start us, length us, event | category | flops | bytes accessed | tf_op | source)
XLA Modules:
  0.0 94.7 jit_solution(10796250206045656635)
XLA Ops:
  0.6 91.5 %shard_map.126 = (bf16[256,512]{1,0:T(8,128)(2,1)S(1)}, f32[256,512]{1,0:T(8,128)S(1)}, f32[1024,256]{1,0:T(8,128)S(1)}, f32[1024,256]{1,0:T(8,128)S(1)}, f32[10...) custom-call(bf16[256,512]{1,0:T(8,128)(2,1)} %refs_0_.1, bf16[4096,256]{1,0:T(8,128)(2,1)} %refs_1_.1, ...), custom_call_target="tpu_custom_call" | custom-call | tf_op jit(solution)/shard_map/pallas_call | solution.py:708
  92.2 2.4 %shard_map.127 = (bf16[256,512]{1,0:T(8,128)(2,1)}, f32[256,512]{1,0:T(8,128)}, f32[1024,256]{1,0:T(8,128)}, f32[1024,256]{1,0:T(8,128)}, f32[1024,256]{1,0:T(8,...) custom-call(bf16[256,512]{1,0:T(8,128)(2,1)S(1)} %get-tuple-element.14.refs_0_, ...), custom_call_target="tpu_custom_call" | custom-call | tf_op jit(solution)/shard_map/pallas_call | solution.py:738

commit v3 on v2

--- a/solution.py
+++ b/solution.py
@@ -33,11 +33,11 @@
 
 
 def result_parts(rows):
-    return parts(rows, ((1, 10), (0, 6)))
+    return parts(rows, ((1, 9), (0, 7)))
 
 
 def input_parts(rows):
-    return parts(rows, ((0, 7), (0, 7), (1, 2)))
+    return parts(rows, ((0, 8), (0, 8)))
 
 
 def inner_size(count):
@@ -58,25 +58,60 @@
         return self.device(self.place + (1 if way == 0 else -1))
 
 
+def outer_sems(order, outer, inner):
+    return outer + 1 if order == 0 else outer * inner + inner
+
+
+def inner_sems(order, outer, inner):
+    if inner == 2:
+        return outer if order == 0 else 1
+    return outer * inner + outer if order == 0 else inner + 1
+
+
+def gather_sems(order, outer, inner):
+    return outer * inner + outer_sems(order, outer, inner) + inner_sems(order, outer, inner)
+
+
+def scatter_sems(order, outer, inner):
+    first, second = (inner, outer) if order == 0 else (outer, inner)
+    return second * (2 * first + 1) + 2 * second + 1
+
+
 class Gather:
-    def __init__(self, source, slots, recv, sent_outer, sent_inner, outer, inner, parts, seen):
-        self.source, self.slots, self.recv = source, slots, recv
-        self.sent_outer, self.sent_inner = sent_outer, sent_inner
+    def __init__(self, source, slots, sems, outer, inner, parts, seen):
+        self.source, self.slots, self.sems = source, slots, sems
         self.outer, self.inner, self.seen = outer, inner, seen
-        self.parts = [(number, *part) for number, part in enumerate(parts)]
+        self.parts, base = [], 0
+        for order, start, rows in parts:
+            self.parts.append((base, order, start, rows))
+            base += gather_sems(order, outer.size, inner.size)
 
     def slot(self, place_outer, place_inner):
         return place_outer * self.inner.size + place_inner
 
     def copy(self, part, slot, line, way, source=None):
-        number, _, start, rows = part
-        sent = self.sent_outer if line is self.outer else self.sent_inner
+        base, order, start, rows = part
+        row, place = slot // self.inner.size, slot % self.inner.size
+        sent = base + self.outer.size * self.inner.size
+        if line is self.outer:
+            if order == 0:
+                twice, once, more = row == line.place, row, line.size
+            else:
+                twice, once, more = row == line.place, slot, line.size * self.inner.size + place
+        else:
+            sent += outer_sems(order, self.outer.size, self.inner.size)
+            index = row if order == 0 else 0
+            if line.size > 2:
+                index = slot if order == 0 else place
+            more = index if line.size == 2 else (line.size * self.outer.size + row if order == 0 else line.size)
+            twice, once = place == line.place, index
+        sent += jnp.where(twice, more, once) if way == 1 else once
         piece = self.slots.at[slot, pl.ds(start, rows)]
         return pltpu.make_async_remote_copy(
             src_ref=piece if source is None else source.at[pl.ds(start, rows)],
             dst_ref=piece,
-            send_sem=sent.at[number, slot, way],
-            recv_sem=self.recv.at[number, slot],
+            send_sem=self.sems.at[sent],
+            recv_sem=self.sems.at[base + slot],
             device_id=line.next(way),
             device_id_type=MESH,
         )
@@ -87,9 +122,9 @@
             self.copy(part, slot, line, way, source).start()
 
     def arrive(self, part, slot):
-        number, _, start, rows = part
+        base, _, start, rows = part
         piece = self.slots.at[slot, pl.ds(start, rows)]
-        pltpu.make_async_copy(piece, piece, self.recv.at[number, slot]).wait()
+        pltpu.make_async_copy(piece, piece, self.sems.at[base + slot]).wait()
 
     def own(self, line, orders=(0, 1)):
         slot = self.slot(self.outer.place, self.inner.place)
@@ -185,15 +220,19 @@
 
 
 class Reduce:
-    def __init__(self, line, term, landed, sems):
-        self.line, self.term, self.landed, self.sems = line, term, landed, sems
+    def __init__(self, line, term, landed, sems, base):
+        self.line, self.term, self.landed, self.sems, self.base = line, term, landed, sems, base
+
+    def landing(self, way, owner, place):
+        index = self.base + self.line.size + owner
+        return self.sems.at[index if way == 0 else jnp.where(owner == place, self.base + 2 * self.line.size, index)]
 
     def copy(self, way, owner):
         return pltpu.make_async_remote_copy(
             src_ref=self.term(owner),
             dst_ref=self.landed(way, owner),
-            send_sem=self.sems(0, way, owner),
-            recv_sem=self.sems(1, way, owner),
+            send_sem=self.sems.at[self.base + owner],
+            recv_sem=self.landing(way, owner, self.line.place + (1 if way == 0 else -1)),
             device_id=self.line.next(way),
             device_id_type=MESH,
         )
@@ -202,7 +241,7 @@
         @pl.when(self.line.has(1 - way))
         def _():
             piece = self.landed(way, owner)
-            pltpu.make_async_copy(piece, piece, self.sems(1, way, owner)).wait()
+            pltpu.make_async_copy(piece, piece, self.landing(way, owner, self.line.place)).wait()
             act(piece[...].astype(WIDE))
 
     def add(self, way, owner):
@@ -234,26 +273,33 @@
     def __init__(self, terms, landed, sems, outer, inner, parts):
         self.terms, self.landed, self.sems = terms, landed, sems
         self.outer, self.inner = outer, inner
-        self.parts = [(number, *part) for number, part in enumerate(parts)]
+        self.parts, base = [], 0
+        for order, start, rows in parts:
+            self.parts.append((base, order, start, rows))
+            base += scatter_sems(order, outer.size, inner.size)
 
     def along_outer(self, part, place):
-        number, _, start, rows = part
+        base, order, start, rows = part
         span = pl.ds(start, rows)
+        base += self.outer.size * (2 * self.inner.size + 1) if order == 0 else place * (2 * self.outer.size + 1)
         return Reduce(
             self.outer,
             lambda owner: self.terms.at[owner, place, span],
             lambda way, owner: self.landed.at[0, way, owner, place, span],
-            lambda end, way, owner: self.sems.at[number, 0, end, way, owner, place],
+            self.sems,
+            base,
         )
 
     def along_inner(self, part, row):
-        number, _, start, rows = part
+        base, order, start, rows = part
         span = pl.ds(start, rows)
+        base += self.inner.size * (2 * self.outer.size + 1) if order == 1 else row * (2 * self.inner.size + 1)
         return Reduce(
             self.inner,
             lambda owner: self.terms.at[row, owner, span],
             lambda way, owner: self.landed.at[1, way, row, owner, span],
-            lambda end, way, owner: self.sems.at[number, 1, end, way, row, owner],
+            self.sems,
+            base,
         )
 
     def steps_inner(self, part, row):
@@ -328,10 +374,7 @@
     fore, rear, grads, normed,
     terms, terms_landed, inputs, inputs_landed, outers, outers_landed, total, total_wo,
     load_sem, fore_sem, rear_sem,
-    tok_recv, tok_outer, tok_inner, tok_moved, tok_landed,
-    cot_recv, cot_outer, cot_inner,
-    grads_recv, grads_outer, grads_inner,
-    terms_sem, inputs_sem, outers_sem,
+    tok_sem, tok_moved, tok_landed, cot_sem, grads_sem, terms_sem, inputs_sem, outers_sem,
 ):
     seq, head = sizes
     head_inner, seq_inner = inner_size(head), inner_size(seq)
@@ -436,12 +479,10 @@
             place = z + (2 * side - 1) * distance
             pl.when((place >= 0) & (place < head_outer) & ((distance > 0) | (side == 0)))(lambda: act(place))
 
-    tok_gather = Gather(tokens_in, tok, tok_recv, tok_outer, tok_inner, outer, inner, gather_parts(rows), project)
-    cot_gather = Gather(cot_in, cot, cot_recv, cot_outer, cot_inner, outer, inner, gather_parts(rows), pull)
+    tok_gather = Gather(tokens_in, tok, tok_sem, outer, inner, gather_parts(rows), project)
+    cot_gather = Gather(cot_in, cot, cot_sem, outer, inner, gather_parts(rows), pull)
     nothing = lambda slot: None
-    grads_gather = Gather(
-        grads.at[s], grads, grads_recv, grads_outer, grads_inner, chip, core, ((0, 0, rows),), nothing
-    )
+    grads_gather = Gather(grads.at[s], grads, grads_sem, chip, core, ((0, 0, rows),), nothing)
 
     tok_gather.own(inner, (1,))
     tok_gather.own(outer)
@@ -512,7 +553,8 @@
         load.wait()
     move_tok_late()
     pull(h)
-    cot_gather.from_outer(1)
+    at_end = (z == 0) | (z == head_outer - 1)
+    pl.when(jnp.logical_not(at_end))(lambda: cot_gather.from_outer(1))
 
     below = lax.broadcasted_iota(jnp.int32, (rows, rows), 1) <= lax.broadcasted_iota(jnp.int32, (rows, rows), 0)
     above = lax.broadcasted_iota(jnp.int32, (rows, rows), 1) >= lax.broadcasted_iota(jnp.int32, (rows, rows), 0)
@@ -532,13 +574,22 @@
         inv_norm = lax.rsqrt(jnp.mean(whole * whole, axis=-1, keepdims=True) + EPSILON)
         normed[:, number * DH : (number + 1) * DH] = (whole * inv_norm).astype(HALF)
 
-    @pl.loop(0, head)
-    def _(slot):
-        span = pl.ds(pl.multiple_of(slot * wide, wide), wide)
-        terms[slot // head_inner, slot % head_inner] = mul(normed[...], wo[:, span]).astype(HALF)
-
     result_sums = Scatter(terms, terms_landed, terms_sem, outer, inner, result_parts(rows))
+
+    def result_terms(row):
+        @pl.loop(0, head_inner)
+        def _(place):
+            span = pl.ds(pl.multiple_of((row * head_inner + place) * wide, wide), wide)
+            terms[row, place] = mul(normed[...], wo[:, span]).astype(HALF)
+
+    each_row(head_outer - 1, result_terms)
     result_sums.outer_first(head_outer - 1)
+
+    @pl.loop(1, head_outer)
+    def _(turn):
+        each_row(head_outer - 1 - turn, result_terms)
+
+    pl.when(at_end)(lambda: cot_gather.from_outer(1))
     cot_gather.from_inner(0)
     for distance in range(2, head_outer):
         cot_gather.from_outer(distance)
@@ -551,6 +602,8 @@
         each_row(head_outer - 1 - turn, result_sums.start_row)
 
     cot_gather.from_inner(head_outer - 2)
+    if head_outer > 2:
+        result_sums.outer_first(1)
     cot_gather.from_inner(head_outer - 1)
 
     for number in range(heads_here):
@@ -585,7 +638,6 @@
     tok_gather.finish()
     finish_tok()
     finish_fore()
-    result_sums.outer_first(1)
     arrive_rear()
     for number in range(heads_here):
         later = jnp.zeros((DH, DH), WIDE)
@@ -639,34 +691,44 @@
         target[...] = jnp.zeros_like(target)
     for distance in range(seq_outer - 1, 0, -1):
         outer_grads.outer_second(distance)
+    for distance in range(head_outer - 2, 1, -1):
+        result_sums.outer_second(distance)
+    for distance in range(head_outer - 2, 0, -1):
+        input_sums.outer_first(distance)
+    weight_grads(s)
+    grads_gather.from_inner(0)
+
+    @pl.loop(1, seq_inner)
+    def _(step):
+        weight_grads(chip.place * seq_inner + (core.place + step) % seq_inner)
+
     input_sums.outer_second(head_outer - 1)
+    if head_outer > 2:
+        result_sums.outer_second(1)
     for distance in range(head_outer - 2, 0, -1):
-        result_sums.outer_second(distance)
-        input_sums.outer_first(distance)
         input_sums.outer_second(distance)
         if distance == head_outer - 2:
             grads_gather.from_outer(1)
-            grads_gather.from_inner(0)
     for distance in range(2, seq_outer):
         grads_gather.from_outer(distance)
         grads_gather.from_inner(distance - 1)
     result_sums.turn()
     input_sums.turn()
-    weight_grads(s)
     grads_gather.from_inner(seq_outer - 1)
 
-    @pl.loop(1, seq)
-    def _(other):
-        weight_grads((s + other) % seq)
+    @pl.loop(seq_inner, seq)
+    def _(step):
+        place = (chip.place + step // seq_inner) % seq_outer
+        weight_grads(place * seq_inner + step % seq_inner)
 
     outer_grads.total(total_wo)
     for number in range(shared):
         grad_wo[:, number * wide : (number + 1) * wide] = total_wo[number * columns : (number + 1) * columns, :]
+    result_sums.total(total)
+    result[...] = total[...].astype(HALF)
     cot_gather.finish()
     finish_rear()
     outer_grads.finish()
-    result_sums.total(total)
-    result[...] = total[...].astype(HALF)
     input_sums.total(grad_tokens)
     for one in (grads_gather, result_sums, input_sums):
         one.finish()
@@ -695,11 +757,8 @@
         vmem = lambda *shape: pltpu.VMEM(shape, HALF)
         full = lambda *shape: pltpu.VMEM(shape, WIDE)
         dma = lambda *shape: pltpu.SemaphoreType.DMA(shape)
-        pieces = len(gather_parts(rows))
-        gathers = lambda: [
-            dma(pieces, head), dma(pieces, head, 2), dma(pieces, head, 2)
-        ]
-        spans = lambda: [dma(1, seq), dma(1, seq, 2), dma(1, seq, 2)]
+        gathers = dma(sum(gather_sems(order, head_outer, head_inner) for order, *_ in gather_parts(rows)))
+        sums = lambda parts: dma(sum(scatter_sems(order, head_outer, head_inner) for order, *_ in parts))
         outs = [
             ((rows, wide), HALF), ((rows, wide), WIDE),
             ((shared * wide, columns), WIDE), ((shared * wide, columns), WIDE), ((shared * wide, columns), WIDE),
@@ -726,10 +785,8 @@
                 vmem(2, 2, seq_outer, seq_inner, shared * columns, wide),
                 full(rows, wide), full(shared * columns, wide),
                 dma(7), dma(2, seq), dma(2, seq),
-                *gathers(), dma(head), dma(seq, shared), *gathers(), *spans(),
-                dma(len(result_parts(rows)), 2, 2, 2, head_outer, head_inner),
-                dma(len(input_parts(rows)), 2, 2, 2, head_outer, head_inner),
-                dma(1, 2, 2, 2, seq_outer, seq_inner),
+                gathers, dma(head), dma(seq, shared), gathers, dma(gather_sems(0, seq_outer, seq_inner)),
+                sums(result_parts(rows)), sums(input_parts(rows)), dma(scatter_sems(0, seq_outer, seq_inner)),
             ],
             compiler_params=pltpu.CompilerParams(
                 collective_id=0, has_side_effects=True, vmem_limit_bytes=54 * 1024 * 1024

time: 95.2 us -> 92 us (0.966)
  the two profiles are of different devices: /device:TPU:10 before, /device:TPU:0 now
where the time goes in v3:
time: 92 us; the launch traced here: 91.9 us
  Pallas kernels  91.1 us (99%)
    pallas_call x1, Pallas kernels, on_device(): pl.pallas_call(lambda *refs: layer((seq, head), *refs), out_shape=[pltpu....  88.7 us
    pallas_call x1, Pallas kernels, on_device(): pl.pallas_call(write_out, out_shape=[jax.ShapeDtypeStruct(shape, kind) fo...  2.36 us

profile of v3, /device:TPU:0, one launch (start us, length us, event | category | flops | bytes accessed | tf_op | source)
XLA Modules:
  0.0 91.9 jit_solution(7180796915659472869)
XLA Ops:
  0.6 88.7 %shard_map.126 = (bf16[256,512]{1,0:T(8,128)(2,1)S(1)}, f32[256,512]{1,0:T(8,128)S(1)}, f32[1024,256]{1,0:T(8,128)S(1)}, f32[1024,256]{1,0:T(8,128)S(1)}, f32[10...) custom-call(bf16[256,512]{1,0:T(8,128)(2,1)} %refs_0_.1, bf16[4096,256]{1,0:T(8,128)(2,1)} %refs_1_.1, ...), custom_call_target="tpu_custom_call" | custom-call | tf_op jit(solution)/shard_map/pallas_call | solution.py:767
  89.3 2.4 %shard_map.127 = (bf16[256,512]{1,0:T(8,128)(2,1)}, f32[256,512]{1,0:T(8,128)}, f32[1024,256]{1,0:T(8,128)}, f32[1024,256]{1,0:T(8,128)}, f32[1024,256]{1,0:T(8,...) custom-call(bf16[256,512]{1,0:T(8,128)(2,1)S(1)} %get-tuple-element.14.refs_0_, ...), custom_call_target="tpu_custom_call" | custom-call | tf_op jit(solution)/shard_map/pallas_call | solution.py:795

commit v4 on v3

--- a/solution.py
+++ b/solution.py
@@ -33,11 +33,11 @@
 
 
 def result_parts(rows):
-    return parts(rows, ((1, 9), (0, 7)))
+    return parts(rows, ((1, 10), (0, 6)))
 
 
 def input_parts(rows):
-    return parts(rows, ((0, 8), (0, 8)))
+    return parts(rows, ((0, 7), (0, 7), (1, 2)))
 
 
 def inner_size(count):
@@ -585,25 +585,23 @@
     each_row(head_outer - 1, result_terms)
     result_sums.outer_first(head_outer - 1)
 
-    @pl.loop(1, head_outer)
-    def _(turn):
-        each_row(head_outer - 1 - turn, result_terms)
-
+    for distance in range(head_outer - 2, 0, -1):
+        each_row(distance, result_terms)
+        pl.when(at_end)(lambda: result_sums.outer_first(distance))
+    each_row(0, result_terms)
     pl.when(at_end)(lambda: cot_gather.from_outer(1))
     cot_gather.from_inner(0)
     for distance in range(2, head_outer):
         cot_gather.from_outer(distance)
         if distance < head_outer - 1:
             cot_gather.from_inner(distance - 1)
-            result_sums.outer_first(head_outer - distance)
+            pl.when(jnp.logical_not(at_end))(lambda: result_sums.outer_first(head_outer - distance))
 
     @pl.loop(0, head_outer)
     def _(turn):
         each_row(head_outer - 1 - turn, result_sums.start_row)
 
     cot_gather.from_inner(head_outer - 2)
-    if head_outer > 2:
-        result_sums.outer_first(1)
     cot_gather.from_inner(head_outer - 1)
 
     for number in range(heads_here):
@@ -634,6 +632,8 @@
         acc[0, :, span] = mul(grad_scores, keys_h) + mul(grad_mixed, prior[number], NT)
         acc[1, :, span] = mul(grad_scores_t, query_h)
         acc[2, :, span] = mul(scores_t[number], grad_mixed)
+    if head_outer > 2:
+        pl.when(jnp.logical_not(at_end))(lambda: result_sums.outer_first(1))
     result_sums.outer_second(head_outer - 1)
     tok_gather.finish()
     finish_tok()
@@ -675,9 +675,10 @@
     grads_gather.own(chip)
     grads_gather.own(core)
 
-    @pl.loop(1, head_outer)
-    def _(turn):
-        each_row(head_outer - 1 - turn, input_terms)
+    for distance in range(head_outer - 2, 0, -1):
+        each_row(distance, input_terms)
+        pl.when(at_end)(lambda: input_sums.outer_first(distance))
+    each_row(0, input_terms)
 
     def weight_grads(place):
         for number in range(shared):
@@ -693,8 +694,6 @@
         outer_grads.outer_second(distance)
     for distance in range(head_outer - 2, 1, -1):
         result_sums.outer_second(distance)
-    for distance in range(head_outer - 2, 0, -1):
-        input_sums.outer_first(distance)
     weight_grads(s)
     grads_gather.from_inner(0)
 
@@ -705,6 +704,8 @@
     input_sums.outer_second(head_outer - 1)
     if head_outer > 2:
         result_sums.outer_second(1)
+    for distance in range(head_outer - 2, 0, -1):
+        pl.when(jnp.logical_not(at_end))(lambda: input_sums.outer_first(distance))
     for distance in range(head_outer - 2, 0, -1):
         input_sums.outer_second(distance)
         if distance == head_outer - 2:

time: 92 us -> 90.5 us (0.984)
  the two profiles are of different devices: /device:TPU:0 before, /device:TPU:10 now
where the time goes in v4:
time: 90.5 us; the launch traced here: 89.6 us
  Pallas kernels  88.8 us (98%)
    pallas_call x1, Pallas kernels, on_device(): pl.pallas_call(lambda *refs: layer((seq, head), *refs), out_shape=[pltpu....  86.5 us
    pallas_call x1, Pallas kernels, on_device(): pl.pallas_call(write_out, out_shape=[jax.ShapeDtypeStruct(shape, kind) fo...  2.36 us

profile of v4, /device:TPU:10, one launch (start us, length us, event | category | flops | bytes accessed | tf_op | source)
XLA Modules:
  0.0 89.6 jit_solution(11521004117388927204)
XLA Ops:
  0.6 86.5 %shard_map.126 = (bf16[256,512]{1,0:T(8,128)(2,1)S(1)}, f32[256,512]{1,0:T(8,128)S(1)}, f32[1024,256]{1,0:T(8,128)S(1)}, f32[1024,256]{1,0:T(8,128)S(1)}, f32[10...) custom-call(bf16[256,512]{1,0:T(8,128)(2,1)} %refs_0_.1, bf16[4096,256]{1,0:T(8,128)(2,1)} %refs_1_.1, ...), custom_call_target="tpu_custom_call" | custom-call | tf_op jit(solution)/shard_map/pallas_call | solution.py:768
  87.1 2.4 %shard_map.127 = (bf16[256,512]{1,0:T(8,128)(2,1)}, f32[256,512]{1,0:T(8,128)}, f32[1024,256]{1,0:T(8,128)}, f32[1024,256]{1,0:T(8,128)}, f32[1024,256]{1,0:T(8,...) custom-call(bf16[256,512]{1,0:T(8,128)(2,1)S(1)} %get-tuple-element.14.refs_0_, ...), custom_call_target="tpu_custom_call" | custom-call | tf_op jit(solution)/shard_map/pallas_call | solution.py:796

commit v5 on v4

--- a/solution.py
+++ b/solution.py
@@ -32,6 +32,10 @@
     return parts(rows, ((0, 7), (0, 6), (1, 3)))
 
 
+def cot_parts(rows):
+    return parts(rows, ((0, 7), (0, 6), (1, 3)))
+
+
 def result_parts(rows):
     return parts(rows, ((1, 10), (0, 6)))
 
@@ -58,54 +62,31 @@
         return self.device(self.place + (1 if way == 0 else -1))
 
 
-def outer_sems(order, outer, inner):
-    return outer + 1 if order == 0 else outer * inner + inner
-
-
-def inner_sems(order, outer, inner):
-    if inner == 2:
-        return outer if order == 0 else 1
-    return outer * inner + outer if order == 0 else inner + 1
-
-
-def gather_sems(order, outer, inner):
-    return outer * inner + outer_sems(order, outer, inner) + inner_sems(order, outer, inner)
-
-
-def scatter_sems(order, outer, inner):
-    first, second = (inner, outer) if order == 0 else (outer, inner)
-    return second * (2 * first + 1) + 2 * second + 1
+def gather_sems(count, outer, inner):
+    return count * outer * inner + 4
+
+
+def scatter_sems(parts, outer, inner):
+    total = 4
+    for order, *_ in parts:
+        first, second = (inner, outer) if order == 0 else (outer, inner)
+        total += second * (first + 1) + second + 1
+    return total
 
 
 class Gather:
     def __init__(self, source, slots, sems, outer, inner, parts, seen):
         self.source, self.slots, self.sems = source, slots, sems
         self.outer, self.inner, self.seen = outer, inner, seen
-        self.parts, base = [], 0
-        for order, start, rows in parts:
-            self.parts.append((base, order, start, rows))
-            base += gather_sems(order, outer.size, inner.size)
+        self.parts = [(number * outer.size * inner.size, *part) for number, part in enumerate(parts)]
+        self.sent = len(parts) * outer.size * inner.size
 
     def slot(self, place_outer, place_inner):
         return place_outer * self.inner.size + place_inner
 
     def copy(self, part, slot, line, way, source=None):
-        base, order, start, rows = part
-        row, place = slot // self.inner.size, slot % self.inner.size
-        sent = base + self.outer.size * self.inner.size
-        if line is self.outer:
-            if order == 0:
-                twice, once, more = row == line.place, row, line.size
-            else:
-                twice, once, more = row == line.place, slot, line.size * self.inner.size + place
-        else:
-            sent += outer_sems(order, self.outer.size, self.inner.size)
-            index = row if order == 0 else 0
-            if line.size > 2:
-                index = slot if order == 0 else place
-            more = index if line.size == 2 else (line.size * self.outer.size + row if order == 0 else line.size)
-            twice, once = place == line.place, index
-        sent += jnp.where(twice, more, once) if way == 1 else once
+        base, _, start, rows = part
+        sent = self.sent + way + (0 if line is self.outer else 2)
         piece = self.slots.at[slot, pl.ds(start, rows)]
         return pltpu.make_async_remote_copy(
             src_ref=piece if source is None else source.at[pl.ds(start, rows)],
@@ -220,18 +201,18 @@
 
 
 class Reduce:
-    def __init__(self, line, term, landed, sems, base):
-        self.line, self.term, self.landed, self.sems, self.base = line, term, landed, sems, base
+    def __init__(self, line, term, landed, sems, sent, base):
+        self.line, self.term, self.landed, self.sems, self.sent, self.base = line, term, landed, sems, sent, base
 
     def landing(self, way, owner, place):
-        index = self.base + self.line.size + owner
-        return self.sems.at[index if way == 0 else jnp.where(owner == place, self.base + 2 * self.line.size, index)]
+        index = self.base + owner
+        return self.sems.at[index if way == 0 else jnp.where(owner == place, self.base + self.line.size, index)]
 
     def copy(self, way, owner):
         return pltpu.make_async_remote_copy(
             src_ref=self.term(owner),
             dst_ref=self.landed(way, owner),
-            send_sem=self.sems.at[self.base + owner],
+            send_sem=self.sems.at[self.sent + way],
             recv_sem=self.landing(way, owner, self.line.place + (1 if way == 0 else -1)),
             device_id=self.line.next(way),
             device_id_type=MESH,
@@ -273,32 +254,34 @@
     def __init__(self, terms, landed, sems, outer, inner, parts):
         self.terms, self.landed, self.sems = terms, landed, sems
         self.outer, self.inner = outer, inner
-        self.parts, base = [], 0
+        self.parts, base = [], 4
         for order, start, rows in parts:
             self.parts.append((base, order, start, rows))
-            base += scatter_sems(order, outer.size, inner.size)
+            base += scatter_sems([(order,)], outer.size, inner.size) - 4
 
     def along_outer(self, part, place):
         base, order, start, rows = part
         span = pl.ds(start, rows)
-        base += self.outer.size * (2 * self.inner.size + 1) if order == 0 else place * (2 * self.outer.size + 1)
+        base += self.outer.size * (self.inner.size + 1) if order == 0 else place * (self.outer.size + 1)
         return Reduce(
             self.outer,
             lambda owner: self.terms.at[owner, place, span],
             lambda way, owner: self.landed.at[0, way, owner, place, span],
             self.sems,
+            0,
             base,
         )
 
     def along_inner(self, part, row):
         base, order, start, rows = part
         span = pl.ds(start, rows)
-        base += self.inner.size * (2 * self.outer.size + 1) if order == 1 else row * (2 * self.inner.size + 1)
+        base += self.inner.size * (self.outer.size + 1) if order == 1 else row * (self.inner.size + 1)
         return Reduce(
             self.inner,
             lambda owner: self.terms.at[row, owner, span],
             lambda way, owner: self.landed.at[1, way, row, owner, span],
             self.sems,
+            2,
             base,
         )
 
@@ -427,7 +410,7 @@
             return pltpu.make_async_remote_copy(
                 src_ref=slots.at[slot],
                 dst_ref=moved.at[s, slot % shared],
-                send_sem=sent.at[slot],
+                send_sem=sent.at[0],
                 recv_sem=landed.at[s, slot % shared],
                 device_id=(slot // shared, h),
                 device_id_type=MESH,
@@ -480,7 +463,7 @@
             pl.when((place >= 0) & (place < head_outer) & ((distance > 0) | (side == 0)))(lambda: act(place))
 
     tok_gather = Gather(tokens_in, tok, tok_sem, outer, inner, gather_parts(rows), project)
-    cot_gather = Gather(cot_in, cot, cot_sem, outer, inner, gather_parts(rows), pull)
+    cot_gather = Gather(cot_in, cot, cot_sem, outer, inner, cot_parts(rows), pull)
     nothing = lambda slot: None
     grads_gather = Gather(grads.at[s], grads, grads_sem, chip, core, ((0, 0, rows),), nothing)
 
@@ -523,8 +506,8 @@
             return pltpu.make_async_remote_copy(
                 src_ref=states.at[s],
                 dst_ref=states.at[s],
-                send_sem=sems.at[0, other],
-                recv_sem=sems.at[1, s],
+                send_sem=sems.at[seq],
+                recv_sem=sems.at[s],
                 device_id=(other, h),
                 device_id_type=MESH,
             )
@@ -538,7 +521,7 @@
 
                 @pl.when((other != s) & wanted(other, s))
                 def _():
-                    pltpu.make_async_copy(states.at[other], states.at[other], sems.at[1, other]).wait()
+                    pltpu.make_async_copy(states.at[other], states.at[other], sems.at[other]).wait()
 
         def finish():
             for other in range(seq):
@@ -758,8 +741,8 @@
         vmem = lambda *shape: pltpu.VMEM(shape, HALF)
         full = lambda *shape: pltpu.VMEM(shape, WIDE)
         dma = lambda *shape: pltpu.SemaphoreType.DMA(shape)
-        gathers = dma(sum(gather_sems(order, head_outer, head_inner) for order, *_ in gather_parts(rows)))
-        sums = lambda parts: dma(sum(scatter_sems(order, head_outer, head_inner) for order, *_ in parts))
+        gathers = lambda parts: dma(gather_sems(len(parts(rows)), head_outer, head_inner))
+        sums = lambda parts: dma(scatter_sems(parts, head_outer, head_inner))
         outs = [
             ((rows, wide), HALF), ((rows, wide), WIDE),
             ((shared * wide, columns), WIDE), ((shared * wide, columns), WIDE), ((shared * wide, columns), WIDE),
@@ -785,9 +768,9 @@
                 vmem(seq_outer, seq_inner, shared * columns, wide),
                 vmem(2, 2, seq_outer, seq_inner, shared * columns, wide),
                 full(rows, wide), full(shared * columns, wide),
-                dma(7), dma(2, seq), dma(2, seq),
-                gathers, dma(head), dma(seq, shared), gathers, dma(gather_sems(0, seq_outer, seq_inner)),
-                sums(result_parts(rows)), sums(input_parts(rows)), dma(scatter_sems(0, seq_outer, seq_inner)),
+                dma(7), dma(seq + 1), dma(seq + 1),
+                gathers(gather_parts), dma(1), dma(seq, shared), gathers(cot_parts), dma(gather_sems(1, seq_outer, seq_inner)),
+                sums(result_parts(rows)), sums(input_parts(rows)), dma(scatter_sems([(0,)], seq_outer, seq_inner)),
             ],
             compiler_params=pltpu.CompilerParams(
                 collective_id=0, has_side_effects=True, vmem_limit_bytes=54 * 1024 * 1024

time: 90.5 us -> 89.5 us (0.989)
  Pallas kernels: 88.8 us -> 87.6 us
    pallas_call x1, Pallas kernels: 86.5 us -> 85.3 us  [on_device(): pl.pallas_call(lambda *refs: layer((seq, head), *refs), out_shape=[pltpu....]
where the time goes in v5:
time: 89.5 us; the launch traced here: 88.4 us
  Pallas kernels  87.6 us (98%)
    pallas_call x1, Pallas kernels, on_device(): pl.pallas_call(lambda *refs: layer((seq, head), *refs), out_shape=[pltpu....  85.3 us
    pallas_call x1, Pallas kernels, on_device(): pl.pallas_call(write_out, out_shape=[jax.ShapeDtypeStruct(shape, kind) fo...  2.36 us

profile of v5, /device:TPU:10, one launch (start us, length us, event | category | flops | bytes accessed | tf_op | source)
XLA Modules:
  0.0 88.4 jit_solution(13546396492424245618)
XLA Ops:
  0.6 85.3 %shard_map.126 = (bf16[256,512]{1,0:T(8,128)(2,1)S(1)}, f32[256,512]{1,0:T(8,128)S(1)}, f32[1024,256]{1,0:T(8,128)S(1)}, f32[1024,256]{1,0:T(8,128)S(1)}, f32[10...) custom-call(bf16[256,512]{1,0:T(8,128)(2,1)} %refs_0_.1, bf16[4096,256]{1,0:T(8,128)(2,1)} %refs_1_.1, ...), custom_call_target="tpu_custom_call" | custom-call | tf_op jit(solution)/shard_map/pallas_call | solution.py:751
  85.9 2.4 %shard_map.127 = (bf16[256,512]{1,0:T(8,128)(2,1)}, f32[256,512]{1,0:T(8,128)}, f32[1024,256]{1,0:T(8,128)}, f32[1024,256]{1,0:T(8,128)}, f32[1024,256]{1,0:T(8,...) custom-call(bf16[256,512]{1,0:T(8,128)(2,1)S(1)} %get-tuple-element.14.refs_0_, ...), custom_call_target="tpu_custom_call" | custom-call | tf_op jit(solution)/shard_map/pallas_call | solution.py:779

commit v6 on v5

--- a/solution.py
+++ b/solution.py
@@ -33,7 +33,7 @@
 
 
 def cot_parts(rows):
-    return parts(rows, ((0, 7), (0, 6), (1, 3)))
+    return parts(rows, ((0, 6), (0, 5), (1, 5)))
 
 
 def result_parts(rows):

time: 89.5 us -> 88.6 us (0.990)
  no operation moved by 1% of the time
where the time goes in v6:
time: 88.6 us; the launch traced here: 88.2 us
  Pallas kernels  87.4 us (99%)
    pallas_call x1, Pallas kernels, on_device(): pl.pallas_call(lambda *refs: layer((seq, head), *refs), out_shape=[pltpu....  85 us
    pallas_call x1, Pallas kernels, on_device(): pl.pallas_call(write_out, out_shape=[jax.ShapeDtypeStruct(shape, kind) fo...  2.36 us

profile of v6, /device:TPU:10, one launch (start us, length us, event | category | flops | bytes accessed | tf_op | source)
XLA Modules:
  0.0 88.2 jit_solution(13775767049887287715)
XLA Ops:
  0.6 85.0 %shard_map.126 = (bf16[256,512]{1,0:T(8,128)(2,1)S(1)}, f32[256,512]{1,0:T(8,128)S(1)}, f32[1024,256]{1,0:T(8,128)S(1)}, f32[1024,256]{1,0:T(8,128)S(1)}, f32[10...) custom-call(bf16[256,512]{1,0:T(8,128)(2,1)} %refs_0_.1, bf16[4096,256]{1,0:T(8,128)(2,1)} %refs_1_.1, ...), custom_call_target="tpu_custom_call" | custom-call | tf_op jit(solution)/shard_map/pallas_call | solution.py:751
  85.6 2.4 %shard_map.127 = (bf16[256,512]{1,0:T(8,128)(2,1)}, f32[256,512]{1,0:T(8,128)}, f32[1024,256]{1,0:T(8,128)}, f32[1024,256]{1,0:T(8,128)}, f32[1024,256]{1,0:T(8,...) custom-call(bf16[256,512]{1,0:T(8,128)(2,1)S(1)} %get-tuple-element.14.refs_0_, ...), custom_call_target="tpu_custom_call" | custom-call | tf_op jit(solution)/shard_map/pallas_call | solution.py:779

commit v7 on v6

--- a/solution.py
+++ b/solution.py
@@ -708,13 +708,14 @@
     outer_grads.total(total_wo)
     for number in range(shared):
         grad_wo[:, number * wide : (number + 1) * wide] = total_wo[number * columns : (number + 1) * columns, :]
-    result_sums.total(total)
-    result[...] = total[...].astype(HALF)
     cot_gather.finish()
     finish_rear()
     outer_grads.finish()
+    grads_gather.finish()
+    result_sums.total(total)
+    result[...] = total[...].astype(HALF)
     input_sums.total(grad_tokens)
-    for one in (grads_gather, result_sums, input_sums):
+    for one in (result_sums, input_sums):
         one.finish()
 
 

time: 88.6 us -> 88.5 us (level)
  no operation moved by 1% of the time
where the time goes in v7:
time: 88.5 us; the launch traced here: 88.1 us
  Pallas kernels  87.3 us (99%)
    pallas_call x1, Pallas kernels, on_device(): pl.pallas_call(lambda *refs: layer((seq, head), *refs), out_shape=[pltpu....  84.9 us
    pallas_call x1, Pallas kernels, on_device(): pl.pallas_call(write_out, out_shape=[jax.ShapeDtypeStruct(shape, kind) fo...  2.36 us

profile of v7, /device:TPU:10, one launch (start us, length us, event | category | flops | bytes accessed | tf_op | source)
XLA Modules:
  0.0 88.1 jit_solution(9169060613741090713)
XLA Ops:
  0.6 84.9 %shard_map.126 = (bf16[256,512]{1,0:T(8,128)(2,1)S(1)}, f32[256,512]{1,0:T(8,128)S(1)}, f32[1024,256]{1,0:T(8,128)S(1)}, f32[1024,256]{1,0:T(8,128)S(1)}, f32[10...) custom-call(bf16[256,512]{1,0:T(8,128)(2,1)} %refs_0_.1, bf16[4096,256]{1,0:T(8,128)(2,1)} %refs_1_.1, ...), custom_call_target="tpu_custom_call" | custom-call | tf_op jit(solution)/shard_map/pallas_call | solution.py:752
  85.6 2.4 %shard_map.127 = (bf16[256,512]{1,0:T(8,128)(2,1)}, f32[256,512]{1,0:T(8,128)}, f32[1024,256]{1,0:T(8,128)}, f32[1024,256]{1,0:T(8,128)}, f32[1024,256]{1,0:T(8,...) custom-call(bf16[256,512]{1,0:T(8,128)(2,1)S(1)} %get-tuple-element.14.refs_0_, ...), custom_call_target="tpu_custom_call" | custom-call | tf_op jit(solution)/shard_map/pallas_call | solution.py:780
